TPU v7x, 256 devices: a whole 4x4x8 slice. The times are simulated.
256 devices in a mesh: pipe: 16 (over y, x), expert: 16 (over z, core).
Axes of the slice: x: 4, y: 4, z: 8, core: 2. Of those that a mesh axis runs over, the one named last changes fastest.
Arguments:
- streams: bfloat16 [16, 2, 1024, 3584], P('pipe', None, 'expert'), may hold values from -6 to 6
- norm_gain: float32 [16, 3584], P('pipe'), may hold values from 0.25 to 1.75
- w_gate: bfloat16 [16, 16, 3584, 512], P('pipe', 'expert'), may hold values from -0.09375 to 0.09375
- w_up: bfloat16 [16, 16, 3584, 512], P('pipe', 'expert'), may hold values from -0.09375 to 0.09375
- w_down: bfloat16 [16, 16, 512, 3584], P('pipe', 'expert'), may hold values from -0.1875 to 0.1875
- routes: int32 [16, 2, 1024, 2], P('pipe', None, 'expert'), may hold values from 0 to 7, all different within a row; in each aligned block of 64 rows (0 to 63, 64 to 127, ..., all dimensions but the last counted through in order) at most 32 rows name the same one
- gate_weights: float32 [16, 2, 1024, 2], P('pipe', None, 'expert'), may hold values from 0.2 to 1.2
Outputs:
- next_streams: bfloat16 [16, 2, 1024, 3584], P('pipe', None, 'expert')
Inputs may be any that keep to these rules, and one draw needn't show every extreme that they name: `routes`: each token names 2 different experts. Within each aligned block of 64 tokens of a micro-batch (the tokens of one device of the expert axis), at most 32 tokens name the same expert, a bound that some block reaches.
All inputs are finite; a program needn't handle non-finite values.
Results may differ from a plain program's by a relative error of at most 0.0051.
Values may be sent and summed in bfloat16 or wider, within the bound.
A program may use at most 128 MiB of HBM per device.

v0:
```python
import jax
import jax.numpy as jnp
from jax import lax
from jax.sharding import PartitionSpec as P


def from_behind(value, axis, steps):
    count = lax.axis_size(axis)
    pairs = [(source, (source + steps) % count) for source in range(count)]
    return lax.ppermute(value, axis, pairs)


def shard_ffn(row_block, gate_local, up_local, down_local):
    gate_val = jnp.dot(row_block, gate_local, preferred_element_type=jnp.float32)
    up_val = jnp.dot(row_block, up_local, preferred_element_type=jnp.float32)
    hidden = (jax.nn.silu(gate_val) * up_val).astype(jnp.bfloat16)
    return jnp.dot(hidden, down_local, preferred_element_type=jnp.float32).astype(jnp.bfloat16)


def expert_pass(outgoing, gate_local, up_local, down_local, shards, capacity, width):
    experts = shards // 2
    outbound = jnp.broadcast_to(outgoing[:, None], (experts, 2, capacity, width)).reshape(
        shards, capacity, width
    )
    arrived = lax.all_to_all(outbound, "expert", split_axis=0, concat_axis=0, tiled=True)
    partial_value = shard_ffn(
        arrived.reshape(shards * capacity, width), gate_local, up_local, down_local
    )
    returned = lax.all_to_all(
        partial_value.reshape(shards, capacity, width),
        "expert",
        split_axis=0,
        concat_axis=0,
        tiled=True,
    )
    paired = returned.reshape(experts, 2, capacity, width)
    return paired[:, 0].astype(jnp.float32) + paired[:, 1].astype(jnp.float32)


def body(streams, norm_gain, w_gate, w_up, w_down, routes, gate_weights):
    shards = lax.axis_size("expert")
    experts = shards // 2
    gate_local = w_gate[0, 0]
    up_local = w_up[0, 0]
    down_local = w_down[0, 0]
    gain_row = norm_gain[0]
    tok_rows = streams.shape[2]
    width = streams.shape[3]
    top_count = routes.shape[3]
    capacity = 2 * tok_rows * top_count // experts
    lane_count = experts * capacity
    lane_index = jnp.arange(lane_count, dtype=jnp.int32)
    expert_index = jnp.arange(experts, dtype=jnp.int32)
    results = []
    for stream in range(2):
        state = streams[0, stream].astype(jnp.float32)
        normed = (
            state * lax.rsqrt(jnp.mean(state * state, axis=-1, keepdims=True) + 1e-06) * gain_row
        ).astype(jnp.bfloat16)
        chosen = routes[0, stream].reshape(-1)
        onehot = (chosen[:, None] == expert_index[None, :]).astype(jnp.int32)
        slot_rank = jnp.sum((jnp.cumsum(onehot, axis=0) - onehot) * onehot, axis=1)
        lane_of = chosen * capacity + slot_rank
        matches = lane_index[:, None] == lane_of[None, :]
        send_matrix = jnp.sum(
            matches.reshape(lane_count, tok_rows, top_count).astype(jnp.float32), axis=-1
        ).astype(jnp.bfloat16)
        outgoing = jnp.dot(send_matrix, normed, preferred_element_type=jnp.float32).astype(
            jnp.bfloat16
        )
        outgoing = outgoing.reshape(experts, capacity, width)
        weights = gate_weights[0, stream].reshape(-1)
        combine = jnp.sum(
            (matches.astype(jnp.float32) * weights[None, :]).reshape(
                lane_count, tok_rows, top_count
            ),
            axis=-1,
        ).T
        expert_rows = expert_pass(
            outgoing, gate_local, up_local, down_local, shards, capacity, width
        )
        mixed = state + jnp.dot(
            combine,
            expert_rows.reshape(lane_count, width),
            precision=lax.Precision.HIGHEST,
            preferred_element_type=jnp.float32,
        )
        results.append(mixed.astype(jnp.bfloat16))
    forward = from_behind(results[0], "pipe", 1)
    backward = from_behind(results[1], "pipe", -1)
    return jnp.stack([forward, backward])[None]


def solution(mesh):
    return jax.shard_map(
        body,
        mesh=mesh,
        in_specs=(
            P("pipe", None, "expert", None),
            P("pipe", None),
            P("pipe", "expert", None, None),
            P("pipe", "expert", None, None),
            P("pipe", "expert", None, None),
            P("pipe", None, "expert", None),
            P("pipe", None, "expert", None),
        ),
        out_specs=P("pipe", None, "expert", None),
        check_vma=False,
    )
```

profile of v0, /device:TPU:30, one launch (start us, length us, event | category | flops | bytes accessed | tf_op | source)
XLA Modules:
  0.0 385.9 jit_solution(10662224006771718337)
XLA Ops:
  0.0 0.7 fusion.52
  1.0 0.2 reduce_window_sum.17
  1.2 0.2 select_reduce_fusion.3
  1.9 0.2 reduce_window_sum.18
  2.5 0.7 slice_bitcast_fusion.1
  3.2 1.4 fusion.24
  4.7 0.7 bitcast_add_fusion.1
  5.4 0.8 reduce
  6.3 1.7 convolution_convert_fusion.2
  8.0 2.2 broadcast_in_dim.13
  10.2 8.7 %all-to-all-start.2 = ((bf16[16,32,3584]{2,1,0:T(8,128)(2,1)}), bf16[16,32,3584]{2,1,0:T(8,128)(2,1)}, u32[]{:S(2)}, u32[]{:S(2)}) async-start(bf16[16,32,3584]{2,1,0:T(8,128)(2,1)} %bitcast.83), calls=%async_computation.2 | async-start | bytes 7340032 | tf_op jit(solution)/shard_map/all_to_all | solution.py:25
  18.9 0.7 convolution_convert_fusion.3
  19.6 82.4 %all-to-all-done.2 = bf16[16,32,3584]{2,1,0:T(8,128)(2,1)} async-done(((bf16[16,32,3584]{2,1,0:T(8,128)(2,1)}), bf16[16,32,3584]{2,1,0:T(8,128)(2,1)}, u32[]{:S(2)}, u32[]{:S(2)}) %all-to-all-start.2) | async-done | bytes 3670048 | tf_op jit(solution)/shard_map/all_to_all | solution.py:25
  102.0 2.3 broadcast_in_dim.11
  104.3 4.8 %all-to-all-start = ((bf16[16,32,3584]{2,1,0:T(8,128)(2,1)}), bf16[16,32,3584]{2,1,0:T(8,128)(2,1)}, u32[]{:S(2)}, u32[]{:S(2)}) async-start(bf16[16,32,3584]{2,1,0:T(8,128)(2,1)} %bitcast.84), calls=%async_computation | async-start | bytes 7340032 | tf_op jit(solution)/shard_map/all_to_all | solution.py:25
  109.1 5.2 %fusion.8 = f32[512,512]{1,0:T(8,128)S(1)} fusion(bf16[512,3584]{1,0:T(8,128)(2,1)} %bitcast.20, bf16[1,1,3584,512]{3,2,1,0:T(8,128)(2,1)} %param.9), kind=kOutput, calls=%fused_computation.14 | convolution fusion | flops 1879048192 | bytes 8388608 | tf_op jit(solution)/shard_map/dot_general | solution.py:14
  114.3 10.1 %convolution_convert_fusion = bf16[512,3584]{1,0:T(8,128)(2,1)} fusion(bf16[1,1,512,3584]{3,2,1,0:T(8,128)(2,1)} %param.11, bf16[512,3584]{1,0:T(8,128)(2,1)} %bitcast.20, bf16[1,1,3584,512]{3,2,1,0:T(8,128)(2,1)} %param.10, f32[512,512]{1,0:T(8,128)S(1)} %fusion.8), kind=kOutput, calls=%fused_computation | convolution fusion | flops 3761504256 | bytes 15728640 | tf_op jit(solution)/shard_map/dot_general | solution.py:17
  124.4 67.8 %all-to-all-done = bf16[16,32,3584]{2,1,0:T(8,128)(2,1)} async-done(((bf16[16,32,3584]{2,1,0:T(8,128)(2,1)}), bf16[16,32,3584]{2,1,0:T(8,128)(2,1)}, u32[]{:S(2)}, u32[]{:S(2)}) %all-to-all-start) | async-done | bytes 3670048 | tf_op jit(solution)/shard_map/all_to_all | solution.py:25
  192.2 4.8 %all-to-all-start.3 = ((bf16[16,32,3584]{2,1,0:T(8,128)(2,1)}), bf16[16,32,3584]{2,1,0:T(8,128)(2,1)}, u32[]{:S(2)}, u32[]{:S(2)}) async-start(bf16[16,32,3584]{2,1,0:T(8,128)(2,1)} %bitcast.88), calls=%async_computation.3 | async-start | bytes 7340032 | tf_op jit(solution)/shard_map/all_to_all | solution.py:29
  196.9 5.2 %fusion.10 = f32[512,512]{1,0:T(8,128)S(1)} fusion(bf16[512,3584]{1,0:T(8,128)(2,1)} %bitcast.6, bf16[1,1,3584,512]{3,2,1,0:T(8,128)(2,1)} %param.9), kind=kOutput, calls=%fused_computation.16 | convolution fusion | flops 1879048192 | bytes 8388608 | tf_op jit(solution)/shard_map/dot_general | solution.py:14
  202.2 10.2 %convolution_convert_fusion.1 = bf16[512,3584]{1,0:T(8,128)(2,1)} fusion(bf16[1,1,512,3584]{3,2,1,0:T(8,128)(2,1)} %param.11, bf16[512,3584]{1,0:T(8,128)(2,1)} %bitcast.6, bf16[1,1,3584,512]{3,2,1,0:T(8,128)(2,1)} %param.10, f32[512,512]{1,0:T(8,128)S(1)} %fusion.10), kind=kOutput, calls=%fused_computation.1 | convolution fusion | flops 3761504256 | bytes 15728640 | tf_op jit(solution)/shard_map/dot_general | solution.py:17
  212.3 67.7 %all-to-all-done.3 = bf16[16,32,3584]{2,1,0:T(8,128)(2,1)} async-done(((bf16[16,32,3584]{2,1,0:T(8,128)(2,1)}), bf16[16,32,3584]{2,1,0:T(8,128)(2,1)}, u32[]{:S(2)}, u32[]{:S(2)}) %all-to-all-start.3) | async-done | bytes 3670048 | tf_op jit(solution)/shard_map/all_to_all | solution.py:29
  280.0 4.8 %all-to-all-start.1 = ((bf16[16,32,3584]{2,1,0:T(8,128)(2,1)}), bf16[16,32,3584]{2,1,0:T(8,128)(2,1)}, u32[]{:S(2)}, u32[]{:S(2)}) async-start(bf16[16,32,3584]{2,1,0:T(8,128)(2,1)} %bitcast.87), calls=%async_computation.1 | async-start | bytes 7340032 | tf_op jit(solution)/shard_map/all_to_all | solution.py:29
  284.8 2.6 convert_add_fusion
  287.4 2.3 fusion.1
  289.7 0.9 collective-permute-start.1
  290.6 77.3 %all-to-all-done.1 = bf16[16,32,3584]{2,1,0:T(8,128)(2,1)} async-done(((bf16[16,32,3584]{2,1,0:T(8,128)(2,1)}), bf16[16,32,3584]{2,1,0:T(8,128)(2,1)}, u32[]{:S(2)}, u32[]{:S(2)}) %all-to-all-start.1) | async-done | bytes 3670048 | tf_op jit(solution)/shard_map/all_to_all | solution.py:29
  367.9 2.6 convert_add_fusion.1
  370.5 2.3 fusion
  372.8 0.2 collective-permute-start
  373.0 11.9 %collective-permute-done = bf16[64,3584]{1,0:T(8,128)(2,1)S(1)} collective-permute-done((bf16[64,3584]{1,0:T(8,128)(2,1)S(1)}, bf16[64,3584]{1,0:T(8,128)(2,1)S(1)}, u32[]{:S(2)}, u32[]{:S(2)}) %collective-permute-start) | collective-permute-done | bytes 458784 | tf_op jit(solution)/shard_map/ppermute | solution.py:10
  384.9 1.0 maximum_bitcast_fusion
  (16 shorter events, 1.4 us)
Async XLA Ops:
  10.2 8.8 %copy-start = (bf16[1,2,64,3584]{3,2,1,0:T(8,128)(2,1)S(1)}, bf16[1,2,64,3584]{3,2,1,0:T(8,128)(2,1)}, u32[]{:S(2)}) copy-start(bf16[1,2,64,3584]{3,2,1,0:T(8,128)(2,1)} %param.7) | copy-start | bytes 2752516
  10.2 91.8 %all-to-all-start.2 = ((bf16[16,32,3584]{2,1,0:T(8,128)(2,1)}), bf16[16,32,3584]{2,1,0:T(8,128)(2,1)}, u32[]{:S(2)}, u32[]{:S(2)}) async-start(bf16[16,32,3584]{2,1,0:T(8,128)(2,1)} %bitcast.83), calls=%async_computation.2 | async-start | bytes 7340032 | tf_op jit(solution)/shard_map/all_to_all | solution.py:25
  104.3 87.9 %all-to-all-start = ((bf16[16,32,3584]{2,1,0:T(8,128)(2,1)}), bf16[16,32,3584]{2,1,0:T(8,128)(2,1)}, u32[]{:S(2)}, u32[]{:S(2)}) async-start(bf16[16,32,3584]{2,1,0:T(8,128)(2,1)} %bitcast.84), calls=%async_computation | async-start | bytes 7340032 | tf_op jit(solution)/shard_map/all_to_all | solution.py:25
  192.2 87.9 %all-to-all-start.3 = ((bf16[16,32,3584]{2,1,0:T(8,128)(2,1)}), bf16[16,32,3584]{2,1,0:T(8,128)(2,1)}, u32[]{:S(2)}, u32[]{:S(2)}) async-start(bf16[16,32,3584]{2,1,0:T(8,128)(2,1)} %bitcast.88), calls=%async_computation.3 | async-start | bytes 7340032 | tf_op jit(solution)/shard_map/all_to_all | solution.py:29
  280.0 87.9 %all-to-all-start.1 = ((bf16[16,32,3584]{2,1,0:T(8,128)(2,1)}), bf16[16,32,3584]{2,1,0:T(8,128)(2,1)}, u32[]{:S(2)}, u32[]{:S(2)}) async-start(bf16[16,32,3584]{2,1,0:T(8,128)(2,1)} %bitcast.87), calls=%async_computation.1 | async-start | bytes 7340032 | tf_op jit(solution)/shard_map/all_to_all | solution.py:29
  289.7 83.3 %collective-permute-start.1 = (bf16[64,3584]{1,0:T(8,128)(2,1)S(1)}, bf16[64,3584]{1,0:T(8,128)(2,1)S(1)}, u32[]{:S(2)}, u32[]{:S(2)}) collective-permute-start(bf16[64,3584]{1,0:T(8,128)(2,1)S(1)} %fusion.1), channel_id=1, source_target_pairs={{0,240},{16,0},{32,16},{48,32},{64,48},{80,64},{96,80},{112,96},{1... | collective-permute-start | bytes 1376264 | tf_op jit(solution)/shard_map/ppermute | solution.py:10
  372.8 12.1 %collective-permute-start = (bf16[64,3584]{1,0:T(8,128)(2,1)S(1)}, bf16[64,3584]{1,0:T(8,128)(2,1)S(1)}, u32[]{:S(2)}, u32[]{:S(2)}) collective-permute-start(bf16[64,3584]{1,0:T(8,128)(2,1)S(1)} %fusion), channel_id=1, source_target_pairs={{0,16},{16,32},{32,48},{48,64},{64,80},{80,96},{96,112},{112,128},... | collective-permute-start | bytes 1376264 | tf_op jit(solution)/shard_map/ppermute | solution.py:10
where the time goes:
time: 390 us; the launch traced here: 386 us
  waiting for transfers between devices  307 us (79%)
  matrix products  37.7 us (10%)
  starting transfers between devices  24.2 us (6%)
  other arithmetic  10.1 us (3%)
  local copies, waits for them, and re-layouts  6.77 us (2%)
    all_to_all x2, waiting for transfers between devices, expert_pass(): lax.all_to_all(outbound, 'expert', split_axis=0, concat_axis=0, tiled=True)  150 us
    all_to_all x2, waiting for transfers between devices, expert_pass(): lax.all_to_all(partial_value.reshape(shards, capacity, width), 'expert',...  145 us
    dot_general x2, matrix products, shard_ffn(): jnp.dot(hidden, down_local, preferred_element_type=jnp.float32)  20.2 us
    all_to_all x2, starting transfers between devices, expert_pass(): lax.all_to_all(outbound, 'expert', split_axis=0, concat_axis=0, tiled=True)  13.5 us
    ppermute x2, waiting for transfers between devices, from_behind(): return lax.ppermute(value, axis, pairs)  11.9 us
    dot_general x2, matrix products, shard_ffn(): jnp.dot(row_block, gate_local, preferred_element_type=jnp.float32)  10.4 us
    all_to_all x2, starting transfers between devices, expert_pass(): lax.all_to_all(partial_value.reshape(shards, capacity, width), 'expert',...  9.54 us
  transfers between devices with their start and end apart: 6, of which 5 were waited for; matrix products, arithmetic and copies ran while one was open for 11% of the time, Pallas kernels for 0%

commit v1 on v0

--- a/solution.py
+++ b/solution.py
@@ -1,6 +1,8 @@
 import jax
 import jax.numpy as jnp
+import numpy as np
 from jax import lax
+from jax.sharding import Mesh
 from jax.sharding import PartitionSpec as P
 
 
@@ -17,29 +19,23 @@
     return jnp.dot(hidden, down_local, preferred_element_type=jnp.float32).astype(jnp.bfloat16)
 
 
-def expert_pass(outgoing, gate_local, up_local, down_local, shards, capacity, width):
-    experts = shards // 2
-    outbound = jnp.broadcast_to(outgoing[:, None], (experts, 2, capacity, width)).reshape(
-        shards, capacity, width
+def expert_pass(outgoing, gate_local, up_local, down_local):
+    chips, capacity, width = outgoing.shape
+    arrived = lax.all_to_all(outgoing, "ez", split_axis=0, concat_axis=0, tiled=True)
+    sibling_rows = from_behind(arrived, "ec", 1)
+    rows = chips * capacity
+    theirs = shard_ffn(sibling_rows.reshape(rows, width), gate_local, up_local, down_local)
+    returned_half = from_behind(theirs, "ec", 1)
+    mine = shard_ffn(arrived.reshape(rows, width), gate_local, up_local, down_local)
+    summed = (mine.astype(jnp.float32) + returned_half.astype(jnp.float32)).astype(jnp.bfloat16)
+    back = lax.all_to_all(
+        summed.reshape(chips, capacity, width), "ez", split_axis=0, concat_axis=0, tiled=True
     )
-    arrived = lax.all_to_all(outbound, "expert", split_axis=0, concat_axis=0, tiled=True)
-    partial_value = shard_ffn(
-        arrived.reshape(shards * capacity, width), gate_local, up_local, down_local
-    )
-    returned = lax.all_to_all(
-        partial_value.reshape(shards, capacity, width),
-        "expert",
-        split_axis=0,
-        concat_axis=0,
-        tiled=True,
-    )
-    paired = returned.reshape(experts, 2, capacity, width)
-    return paired[:, 0].astype(jnp.float32) + paired[:, 1].astype(jnp.float32)
+    return back.astype(jnp.float32)
 
 
 def body(streams, norm_gain, w_gate, w_up, w_down, routes, gate_weights):
-    shards = lax.axis_size("expert")
-    experts = shards // 2
+    experts = lax.axis_size("ez")
     gate_local = w_gate[0, 0]
     up_local = w_up[0, 0]
     down_local = w_down[0, 0]
@@ -76,9 +72,7 @@
             ),
             axis=-1,
         ).T
-        expert_rows = expert_pass(
-            outgoing, gate_local, up_local, down_local, shards, capacity, width
-        )
+        expert_rows = expert_pass(outgoing, gate_local, up_local, down_local)
         mixed = state + jnp.dot(
             combine,
             expert_rows.reshape(lane_count, width),
@@ -92,18 +86,23 @@
 
 
 def solution(mesh):
+    pipe_size, expert_size = mesh.devices.shape
+    split = Mesh(
+        np.asarray(mesh.devices).reshape(pipe_size, expert_size // 2, 2), ("pipe", "ez", "ec")
+    )
+    tok = ("ez", "ec")
     return jax.shard_map(
         body,
-        mesh=mesh,
+        mesh=split,
         in_specs=(
-            P("pipe", None, "expert", None),
+            P("pipe", None, tok, None),
             P("pipe", None),
-            P("pipe", "expert", None, None),
-            P("pipe", "expert", None, None),
-            P("pipe", "expert", None, None),
-            P("pipe", None, "expert", None),
-            P("pipe", None, "expert", None),
+            P("pipe", tok, None, None),
+            P("pipe", tok, None, None),
+            P("pipe", tok, None, None),
+            P("pipe", None, tok, None),
+            P("pipe", None, tok, None),
         ),
-        out_specs=P("pipe", None, "expert", None),
+        out_specs=P("pipe", None, tok, None),
         check_vma=False,
     )

time: 390 us -> 256 us (0.66)
  waiting for transfers between devices: 307 us -> 166 us
  matrix products: 37.7 us -> 55 us
  other arithmetic: 10.1 us -> 4.9 us
    all_to_all x4, waiting for transfers between devices: 295 us -> 157 us  [the longest x2 89.5 us: expert_pass(): lax.all_to_all(outgoing, 'ez', split_axis=0, concat_axis=0, tiled=True)]
    dot_general x2 -> x4, matrix products: 20.2 us -> 29.7 us  [shard_ffn(): jnp.dot(hidden, down_local, preferred_element_type=jnp.float32)]
    dot_general x0 -> x2, matrix products: none -> 8.72 us  [shard_ffn(): up_val = jnp.dot(row_block, up_local, preferred_element_type=jnp.float32)]
    add x2 -> x0, other arithmetic: 5.15 us -> none  [expert_pass(): return paired[:, 0].astype(jnp.float32) + paired[:, 1].astype(jnp.float32)]
    broadcast_in_dim x2 -> x0, local copies, waits for them, and re-layouts: 4.45 us -> none  [expert_pass(): jnp.broadcast_to(outgoing[:, None], (experts, 2, capacity, width))]
    ppermute x2 -> x6, waiting for transfers between devices: 11.9 us -> 9.42 us  [from_behind(): return lax.ppermute(value, axis, pairs)]
  transfers between devices with their start and end apart: 6 -> 10, of which waited for: 5 -> 5; matrix products, arithmetic and copies ran while one was open for 11% -> 18% of each run, Pallas kernels for 0% -> 0%
where the time goes in v1:
time: 256 us; the launch traced here: 252 us
  waiting for transfers between devices  166 us (65%)
  matrix products  55 us (21%)
  starting transfers between devices  22.2 us (9%)
  other arithmetic  4.9 us (2%)
  local copies, waits for them, and re-layouts  3.64 us (1%)
    all_to_all x2, waiting for transfers between devices, expert_pass(): lax.all_to_all(outgoing, 'ez', split_axis=0, concat_axis=0, tiled=True)  89.5 us
    all_to_all x2, waiting for transfers between devices, expert_pass(): lax.all_to_all(summed.reshape(chips, capacity, width), 'ez', split_axis=0...  67.2 us
    dot_general x4, matrix products, shard_ffn(): jnp.dot(hidden, down_local, preferred_element_type=jnp.float32)  29.7 us
    all_to_all x2, starting transfers between devices, expert_pass(): lax.all_to_all(outgoing, 'ez', split_axis=0, concat_axis=0, tiled=True)  12.1 us
    ppermute x6, waiting for transfers between devices, from_behind(): return lax.ppermute(value, axis, pairs)  9.42 us
    dot_general x2, matrix products, shard_ffn(): jnp.dot(row_block, gate_local, preferred_element_type=jnp.float32)  9.14 us
    dot_general x2, matrix products, shard_ffn(): up_val = jnp.dot(row_block, up_local, preferred_element_type=jnp.float32)  8.72 us
    all_to_all x2, starting transfers between devices, expert_pass(): lax.all_to_all(summed.reshape(chips, capacity, width), 'ez', split_axis=0...  8.41 us
  transfers between devices with their start and end apart: 10, of which 5 were waited for; matrix products, arithmetic and copies ran while one was open for 18% of the time, Pallas kernels for 0%

profile of v1, /device:TPU:30, one launch (start us, length us, event | category | flops | bytes accessed | tf_op | source)
XLA Modules:
  0.0 252.0 jit_solution(9125584160833011289)
XLA Ops:
  0.0 0.8 fusion.94
  1.1 0.2 reduce_window_sum.17
  2.6 0.7 slice_bitcast_fusion.1
  3.3 1.4 fusion.48
  4.8 0.7 bitcast_add_fusion.1
  5.5 0.8 reduce
  6.4 1.9 convolution_convert_fusion.2
  8.3 8.5 %all-to-all-start.2 = ((bf16[8,32,3584]{2,1,0:T(8,128)(2,1)}), bf16[8,32,3584]{2,1,0:T(8,128)(2,1)S(1)}, u32[]{:S(2)}, u32[]{:S(2)}) async-start(bf16[8,32,3584]{2,1,0:T(8,128)(2,1)} %bitcast.17), calls=%async_computation.2 | async-start | bytes 3670016 | tf_op jit(solution)/shard_map/all_to_all | solution.py:24
  16.8 2.0 convolution_convert_fusion.5
  18.7 43.6 %all-to-all-done.2 = bf16[8,32,3584]{2,1,0:T(8,128)(2,1)S(1)} async-done(((bf16[8,32,3584]{2,1,0:T(8,128)(2,1)}), bf16[8,32,3584]{2,1,0:T(8,128)(2,1)S(1)}, u32[]{:S(2)}, u32[]{:S(2)}) %all-to-all-start.2) | async-done | bytes 1835040 | tf_op jit(solution)/shard_map/all_to_all | solution.py:24
  62.4 1.2 copy-done.2
  63.6 3.6 %all-to-all-start = ((bf16[8,32,3584]{2,1,0:T(8,128)(2,1)}), bf16[8,32,3584]{2,1,0:T(8,128)(2,1)S(1)}, u32[]{:S(2)}, u32[]{:S(2)}) async-start(bf16[8,32,3584]{2,1,0:T(8,128)(2,1)} %bitcast.4), calls=%async_computation | async-start | bytes 3670016 | tf_op jit(solution)/shard_map/all_to_all | solution.py:24
  67.3 45.9 %all-to-all-done = bf16[8,32,3584]{2,1,0:T(8,128)(2,1)S(1)} async-done(((bf16[8,32,3584]{2,1,0:T(8,128)(2,1)}), bf16[8,32,3584]{2,1,0:T(8,128)(2,1)S(1)}, u32[]{:S(2)}, u32[]{:S(2)}) %all-to-all-start) | async-done | bytes 1835040 | tf_op jit(solution)/shard_map/all_to_all | solution.py:24
  113.1 5.2 %fusion.8 = f32[256,512]{1,0:T(8,128)} fusion(bf16[256,3584]{1,0:T(8,128)(2,1)} %bitcast.19, bf16[1,1,3584,512]{3,2,1,0:T(8,128)(2,1)} %param.10), kind=kOutput, calls=%fused_computation.16 | convolution fusion | flops 939524096 | bytes 6029312 | tf_op jit(solution)/shard_map/dot_general | solution.py:17
  118.3 7.4 %convolution_convert_fusion = bf16[256,3584]{1,0:T(8,128)(2,1)} fusion(bf16[1,1,512,3584]{3,2,1,0:T(8,128)(2,1)} %param.11, f32[256,512]{1,0:T(8,128)} %fusion.8, bf16[256,3584]{1,0:T(8,128)(2,1)} %bitcast.19, bf16[1,1,3584,512]{3,2,1,0:T(8,128)(2,1)} %param.9), kind=kOutput, calls=%fused_computation | convolution fusion | flops 1880752128 | bytes 11534336 | tf_op jit(solution)/shard_map/dot_general | solution.py:19
  125.7 4.6 %fusion.18 = f32[256,512]{1,0:T(8,128)} fusion(bf16[256,3584]{1,0:T(8,128)(2,1)} %bitcast.114, bf16[1,1,3584,512]{3,2,1,0:T(8,128)(2,1)} %param.9), kind=kOutput, calls=%fused_computation.26 | convolution fusion | flops 939524096 | bytes 6029312 | tf_op jit(solution)/shard_map/dot_general | solution.py:16
  130.4 3.6 %fusion.12 = f32[256,512]{1,0:T(8,128)} fusion(bf16[256,3584]{1,0:T(8,128)(2,1)} %bitcast.9, bf16[1,1,3584,512]{3,2,1,0:T(8,128)(2,1)S(1)} %copy-done.4), kind=kOutput, calls=%fused_computation.20 | convolution fusion | flops 939524096 | bytes 6029312 | tf_op jit(solution)/shard_map/dot_general | solution.py:17
  133.9 7.2 %add_convert_fusion = bf16[256,3584]{1,0:T(8,128)(2,1)} fusion(bf16[256,3584]{1,0:T(8,128)(2,1)} %collective-permute-done.4, bf16[1,1,512,3584]{3,2,1,0:T(8,128)(2,1)} %param.11, bf16[256,3584]{1,0:T(8,128)(2,1)S(1)} %bitcast.115, bf16[1,1,3584,512]{3,2,1,0:T(8,128)(2,1)} %param.10, f32[256,512]{1,0:T(8,128)} %fusion.18), kind=kOutput, calls=%fused_computation.32 | convolution fusion | flops 1884422144 | bytes 13369344 | tf_op jit(solution)/shard_map/dot_general | solution.py:19
  141.1 3.6 %all-to-all-start.3 = ((bf16[8,32,3584]{2,1,0:T(8,128)(2,1)}), bf16[8,32,3584]{2,1,0:T(8,128)(2,1)S(1)}, u32[]{:S(2)}, u32[]{:S(2)}) async-start(bf16[8,32,3584]{2,1,0:T(8,128)(2,1)} %bitcast.116), calls=%async_computation.3 | async-start | bytes 3670016 | tf_op jit(solution)/shard_map/all_to_all | solution.py:31
  144.7 7.4 %convolution_convert_fusion.3 = bf16[256,3584]{1,0:T(8,128)(2,1)} fusion(bf16[1,1,512,3584]{3,2,1,0:T(8,128)(2,1)} %param.11, f32[256,512]{1,0:T(8,128)} %fusion.12, bf16[256,3584]{1,0:T(8,128)(2,1)} %bitcast.9, bf16[1,1,3584,512]{3,2,1,0:T(8,128)(2,1)} %param.9), kind=kOutput, calls=%fused_computation.4 | convolution fusion | flops 1880752128 | bytes 11534336 | tf_op jit(solution)/shard_map/dot_general | solution.py:19
  152.1 0.5 collective-permute-start.1
  152.6 4.5 %fusion.22 = f32[256,512]{1,0:T(8,128)} fusion(bf16[256,3584]{1,0:T(8,128)(2,1)} %bitcast.112, bf16[1,1,3584,512]{3,2,1,0:T(8,128)(2,1)} %param.9), kind=kOutput, calls=%fused_computation.30 | convolution fusion | flops 939524096 | bytes 6029312 | tf_op jit(solution)/shard_map/dot_general | solution.py:16
  157.1 7.7 %add_convert_fusion.1 = bf16[256,3584]{1,0:T(8,128)(2,1)} fusion(bf16[256,3584]{1,0:T(8,128)(2,1)} %collective-permute-done.1, bf16[1,1,512,3584]{3,2,1,0:T(8,128)(2,1)} %param.11, bf16[256,3584]{1,0:T(8,128)(2,1)} %bitcast.113, bf16[1,1,3584,512]{3,2,1,0:T(8,128)(2,1)} %param.10, f32[256,512]{1,0:T(8,128)} %fusion.22), kind=kOutput, calls=%fused_computation.33 | convolution fusion | flops 1884422144 | bytes 13369344 | tf_op jit(solution)/shard_map/dot_general | solution.py:19
  164.8 23.5 %all-to-all-done.3 = bf16[8,32,3584]{2,1,0:T(8,128)(2,1)S(1)} async-done(((bf16[8,32,3584]{2,1,0:T(8,128)(2,1)}), bf16[8,32,3584]{2,1,0:T(8,128)(2,1)S(1)}, u32[]{:S(2)}, u32[]{:S(2)}) %all-to-all-start.3) | async-done | bytes 1835040 | tf_op jit(solution)/shard_map/all_to_all | solution.py:31
  188.3 4.8 %all-to-all-start.1 = ((bf16[8,32,3584]{2,1,0:T(8,128)(2,1)}), bf16[8,32,3584]{2,1,0:T(8,128)(2,1)}, u32[]{:S(2)}, u32[]{:S(2)}) async-start(bf16[8,32,3584]{2,1,0:T(8,128)(2,1)} %bitcast.117), calls=%async_computation.1 | async-start | bytes 3670016 | tf_op jit(solution)/shard_map/all_to_all | solution.py:31
  193.1 1.1 fusion.3
  194.2 0.9 collective-permute-start.5
  195.1 43.7 %all-to-all-done.1 = bf16[8,32,3584]{2,1,0:T(8,128)(2,1)} async-done(((bf16[8,32,3584]{2,1,0:T(8,128)(2,1)}), bf16[8,32,3584]{2,1,0:T(8,128)(2,1)}, u32[]{:S(2)}, u32[]{:S(2)}) %all-to-all-start.1) | async-done | bytes 1835040 | tf_op jit(solution)/shard_map/all_to_all | solution.py:31
  238.8 2.6 %fusion.2 = bf16[64,3584]{1,0:T(8,128)(2,1)S(1)} fusion(f32[256,64]{0,1:T(8,128)S(1)} %get-tuple-element.17, bf16[256,3584]{1,0:T(8,128)(2,1)} %bitcast.11, bf16[1,2,64,3584]{3,2,1,0:T(8,128)(2,1)S(1)} %copy-done), kind=kOutput, calls=%fused_computation.10 | convolution fusion | flops 705331200 | bytes 2818048 | tf_op jit(solution)/shard_map/dot_general | solution.py:76
  241.4 0.2 collective-permute-start.2
  241.6 9.4 %collective-permute-done.2 = bf16[64,3584]{1,0:T(8,128)(2,1)S(1)} collective-permute-done((bf16[64,3584]{1,0:T(8,128)(2,1)S(1)}, bf16[64,3584]{1,0:T(8,128)(2,1)S(1)}, u32[]{:S(2)}, u32[]{:S(2)}) %collective-permute-start.2) | collective-permute-done | bytes 458784 | tf_op jit(solution)/shard_map/ppermute | solution.py:12
  251.0 1.0 maximum_bitcast_fusion
  (32 shorter events, 1.9 us)
Async XLA Ops:
  0.0 6.4 %copy-start = (bf16[1,2,64,3584]{3,2,1,0:T(8,128)(2,1)S(1)}, bf16[1,2,64,3584]{3,2,1,0:T(8,128)(2,1)}, u32[]{:S(2)}) copy-start(bf16[1,2,64,3584]{3,2,1,0:T(8,128)(2,1)} %param.7) | copy-start | bytes 2752516
  8.3 54.0 %all-to-all-start.2 = ((bf16[8,32,3584]{2,1,0:T(8,128)(2,1)}), bf16[8,32,3584]{2,1,0:T(8,128)(2,1)S(1)}, u32[]{:S(2)}, u32[]{:S(2)}) async-start(bf16[8,32,3584]{2,1,0:T(8,128)(2,1)} %bitcast.17), calls=%async_computation.2 | async-start | bytes 3670016 | tf_op jit(solution)/shard_map/all_to_all | solution.py:24
  62.3 1.2 copy-start.2
  63.6 49.6 %all-to-all-start = ((bf16[8,32,3584]{2,1,0:T(8,128)(2,1)}), bf16[8,32,3584]{2,1,0:T(8,128)(2,1)S(1)}, u32[]{:S(2)}, u32[]{:S(2)}) async-start(bf16[8,32,3584]{2,1,0:T(8,128)(2,1)} %bitcast.4), calls=%async_computation | async-start | bytes 3670016 | tf_op jit(solution)/shard_map/all_to_all | solution.py:24
  67.2 46.0 %collective-permute-start.3 = (bf16[8,32,3584]{2,1,0:T(8,128)(2,1)}, bf16[8,32,3584]{2,1,0:T(8,128)(2,1)}, u32[]{:S(2)}, u32[]{:S(2)}) collective-permute-start(bf16[8,32,3584]{2,1,0:T(8,128)(2,1)} %copy-done.2), channel_id=1, source_target_pairs={{0,1},{1,0},{2,3},{3,2},{4,5},{5,4},{6,7},{7,6},{8,9},{9,8},{10,11... | collective-permute-start | bytes 5505032 | tf_op jit(solution)/shard_map/ppermute | solution.py:12
  113.1 5.2 %copy-start.1 = (bf16[8,32,3584]{2,1,0:T(8,128)(2,1)}, bf16[8,32,3584]{2,1,0:T(8,128)(2,1)S(1)}, u32[]{:S(2)}) copy-start(bf16[8,32,3584]{2,1,0:T(8,128)(2,1)S(1)} %all-to-all-done) | copy-start | bytes 5505028
  113.1 17.2 %collective-permute-start = (bf16[8,32,3584]{2,1,0:T(8,128)(2,1)S(1)}, bf16[8,32,3584]{2,1,0:T(8,128)(2,1)}, u32[]{:S(2)}, u32[]{:S(2)}) collective-permute-start(bf16[8,32,3584]{2,1,0:T(8,128)(2,1)S(1)} %all-to-all-done), channel_id=1, source_target_pairs={{0,1},{1,0},{2,3},{3,2},{4,5},{5,4},{6,7},{7,6},{8,9},{9,8},{10,11... | collective-permute-start | bytes 5505032 | tf_op jit(solution)/shard_map/ppermute | solution.py:12
  125.7 8.2 %collective-permute-start.4 = (bf16[256,3584]{1,0:T(8,128)(2,1)}, bf16[256,3584]{1,0:T(8,128)(2,1)}, u32[]{:S(2)}, u32[]{:S(2)}) collective-permute-start(bf16[256,3584]{1,0:T(8,128)(2,1)} %convolution_convert_fusion), channel_id=1, source_target_pairs={{0,1},{1,0},{2,3},{3,2},{4,5},{5,4},{6,7},{7,6},{8,9},{9,8},{10,11... | collective-permute-start | bytes 5505032 | tf_op jit(solution)/shard_map/ppermute | solution.py:12
  125.7 4.7 %copy-start.4 = (bf16[1,1,3584,512]{3,2,1,0:T(8,128)(2,1)S(1)}, bf16[1,1,3584,512]{3,2,1,0:T(8,128)(2,1)}, u32[]{:S(2)}) copy-start(bf16[1,1,3584,512]{3,2,1,0:T(8,128)(2,1)} %param.10) | copy-start | bytes 11010052
  130.4 3.6 %copy-start.3 = (bf16[8,32,3584]{2,1,0:T(8,128)(2,1)S(1)}, bf16[8,32,3584]{2,1,0:T(8,128)(2,1)}, u32[]{:S(2)}) copy-start(bf16[8,32,3584]{2,1,0:T(8,128)(2,1)} %copy-done.2) | copy-start | bytes 5505028
  141.1 47.2 %all-to-all-start.3 = ((bf16[8,32,3584]{2,1,0:T(8,128)(2,1)}), bf16[8,32,3584]{2,1,0:T(8,128)(2,1)S(1)}, u32[]{:S(2)}, u32[]{:S(2)}) async-start(bf16[8,32,3584]{2,1,0:T(8,128)(2,1)} %bitcast.116), calls=%async_computation.3 | async-start | bytes 3670016 | tf_op jit(solution)/shard_map/all_to_all | solution.py:31
  152.1 5.0 %collective-permute-start.1 = (bf16[256,3584]{1,0:T(8,128)(2,1)}, bf16[256,3584]{1,0:T(8,128)(2,1)}, u32[]{:S(2)}, u32[]{:S(2)}) collective-permute-start(bf16[256,3584]{1,0:T(8,128)(2,1)} %convolution_convert_fusion.3), channel_id=1, source_target_pairs={{0,1},{1,0},{2,3},{3,2},{4,5},{5,4},{6,7},{7,6},{8,9},{9,8},{10,11... | collective-permute-start | bytes 5505032 | tf_op jit(solution)/shard_map/ppermute | solution.py:12
  188.3 50.5 %all-to-all-start.1 = ((bf16[8,32,3584]{2,1,0:T(8,128)(2,1)}), bf16[8,32,3584]{2,1,0:T(8,128)(2,1)}, u32[]{:S(2)}, u32[]{:S(2)}) async-start(bf16[8,32,3584]{2,1,0:T(8,128)(2,1)} %bitcast.117), calls=%async_computation.1 | async-start | bytes 3670016 | tf_op jit(solution)/shard_map/all_to_all | solution.py:31
  194.2 47.4 %collective-permute-start.5 = (bf16[64,3584]{1,0:T(8,128)(2,1)S(1)}, bf16[64,3584]{1,0:T(8,128)(2,1)S(1)}, u32[]{:S(2)}, u32[]{:S(2)}) collective-permute-start(bf16[64,3584]{1,0:T(8,128)(2,1)S(1)} %fusion.3), channel_id=1, source_target_pairs={{0,240},{16,0},{32,16},{48,32},{64,48},{80,64},{96,80},{112,96},{1... | collective-permute-start | bytes 1376264 | tf_op jit(solution)/shard_map/ppermute | solution.py:12
  241.4 9.6 %collective-permute-start.2 = (bf16[64,3584]{1,0:T(8,128)(2,1)S(1)}, bf16[64,3584]{1,0:T(8,128)(2,1)S(1)}, u32[]{:S(2)}, u32[]{:S(2)}) collective-permute-start(bf16[64,3584]{1,0:T(8,128)(2,1)S(1)} %fusion.2), channel_id=1, source_target_pairs={{0,16},{16,32},{32,48},{48,64},{64,80},{80,96},{96,112},{112,128},... | collective-permute-start | bytes 1376264 | tf_op jit(solution)/shard_map/ppermute | solution.py:12

commit v2 on v1

--- a/solution.py
+++ b/solution.py
@@ -12,22 +12,23 @@
     return lax.ppermute(value, axis, pairs)
 
 
-def shard_ffn(row_block, gate_local, up_local, down_local):
-    gate_val = jnp.dot(row_block, gate_local, preferred_element_type=jnp.float32)
-    up_val = jnp.dot(row_block, up_local, preferred_element_type=jnp.float32)
+def full_ffn(row_block, gate_full, up_full, down_pair):
+    gate_val = jnp.dot(row_block, gate_full, preferred_element_type=jnp.float32)
+    up_val = jnp.dot(row_block, up_full, preferred_element_type=jnp.float32)
     hidden = (jax.nn.silu(gate_val) * up_val).astype(jnp.bfloat16)
-    return jnp.dot(hidden, down_local, preferred_element_type=jnp.float32).astype(jnp.bfloat16)
+    half = down_pair.shape[1]
+    first = jnp.dot(hidden[:, :half], down_pair[0], preferred_element_type=jnp.float32)
+    second = jnp.dot(hidden[:, half:], down_pair[1], preferred_element_type=jnp.float32)
+    summed = first.astype(jnp.bfloat16).astype(jnp.float32) + second.astype(
+        jnp.bfloat16
+    ).astype(jnp.float32)
+    return summed.astype(jnp.bfloat16)
 
 
-def expert_pass(outgoing, gate_local, up_local, down_local):
+def expert_pass(outgoing, gate_full, up_full, down_pair):
     chips, capacity, width = outgoing.shape
     arrived = lax.all_to_all(outgoing, "ez", split_axis=0, concat_axis=0, tiled=True)
-    sibling_rows = from_behind(arrived, "ec", 1)
-    rows = chips * capacity
-    theirs = shard_ffn(sibling_rows.reshape(rows, width), gate_local, up_local, down_local)
-    returned_half = from_behind(theirs, "ec", 1)
-    mine = shard_ffn(arrived.reshape(rows, width), gate_local, up_local, down_local)
-    summed = (mine.astype(jnp.float32) + returned_half.astype(jnp.float32)).astype(jnp.bfloat16)
+    summed = full_ffn(arrived.reshape(chips * capacity, width), gate_full, up_full, down_pair)
     back = lax.all_to_all(
         summed.reshape(chips, capacity, width), "ez", split_axis=0, concat_axis=0, tiled=True
     )
@@ -36,9 +37,9 @@
 
 def body(streams, norm_gain, w_gate, w_up, w_down, routes, gate_weights):
     experts = lax.axis_size("ez")
-    gate_local = w_gate[0, 0]
-    up_local = w_up[0, 0]
-    down_local = w_down[0, 0]
+    gate_full = jnp.concatenate(lax.all_gather(w_gate[0, 0], "ec"), axis=1)
+    up_full = jnp.concatenate(lax.all_gather(w_up[0, 0], "ec"), axis=1)
+    down_pair = lax.all_gather(w_down[0, 0], "ec")
     gain_row = norm_gain[0]
     tok_rows = streams.shape[2]
     width = streams.shape[3]
@@ -72,7 +73,7 @@
             ),
             axis=-1,
         ).T
-        expert_rows = expert_pass(outgoing, gate_local, up_local, down_local)
+        expert_rows = expert_pass(outgoing, gate_full, up_full, down_pair)
         mixed = state + jnp.dot(
             combine,
             expert_rows.reshape(lane_count, width),

time: 256 us -> 242 us (0.945)
  waiting for transfers between devices: 166 us -> 142 us
  local copies, waits for them, and re-layouts: 3.64 us -> 25.2 us
  matrix products: 55 us -> 36.1 us
  between operations: 0.13 us -> 13.4 us
    all_to_all x2, waiting for transfers between devices: 89.5 us -> 54 us  [expert_pass(): lax.all_to_all(outgoing, 'ez', split_axis=0, concat_axis=0, tiled=True)]
    all_gather x0 -> x2, local copies, waits for them, and re-layouts: none -> 20.5 us  [the longest x1 10.4 us: body(): gate_full = jnp.concatenate(lax.all_gather(w_gate[0, 0], 'ec'), axis=1)]
    dot_general x8, matrix products: 47.5 us -> 28.6 us  [the longest x2 11.7 us: full_ffn(): gate_val = jnp.dot(row_block, gate_full, preferred_element_type=jnp.float32)]
    all_to_all x2, waiting for transfers between devices: 67.2 us -> 73.5 us  [expert_pass(): lax.all_to_all(summed.reshape(chips, capacity, width), 'ez', split_axis=0...]
    ppermute x6 -> x2, waiting for transfers between devices: 9.42 us -> 12 us  [from_behind(): return lax.ppermute(value, axis, pairs)]
  transfers between devices with their start and end apart: 10 -> 9, of which waited for: 5 -> 5; matrix products, arithmetic and copies ran while one was open for 18% -> 25% of each run, Pallas kernels for 0% -> 0%
where the time goes in v2:
time: 242 us; the launch traced here: 240 us
  waiting for transfers between devices  142 us (59%)
  matrix products  36.1 us (15%)
  local copies, waits for them, and re-layouts  25.2 us (10%)
  starting transfers between devices  21.3 us (9%)
  between operations  13.4 us (6%)
    all_to_all x2, waiting for transfers between devices, expert_pass(): lax.all_to_all(summed.reshape(chips, capacity, width), 'ez', split_axis=0...  73.5 us
    all_to_all x2, waiting for transfers between devices, expert_pass(): lax.all_to_all(outgoing, 'ez', split_axis=0, concat_axis=0, tiled=True)  54 us
    all_to_all x2, starting transfers between devices, expert_pass(): lax.all_to_all(outgoing, 'ez', split_axis=0, concat_axis=0, tiled=True)  12.1 us
    ppermute x2, waiting for transfers between devices, from_behind(): return lax.ppermute(value, axis, pairs)  12 us
    dot_general x2, matrix products, full_ffn(): gate_val = jnp.dot(row_block, gate_full, preferred_element_type=jnp.float32)  11.7 us
    all_gather x1, local copies, waits for them, and re-layouts, body(): gate_full = jnp.concatenate(lax.all_gather(w_gate[0, 0], 'ec'), axis=1)  10.4 us
    all_gather x1, local copies, waits for them, and re-layouts, body(): up_full = jnp.concatenate(lax.all_gather(w_up[0, 0], 'ec'), axis=1)  10.2 us
    all_to_all x2, starting transfers between devices, expert_pass(): lax.all_to_all(summed.reshape(chips, capacity, width), 'ez', split_axis=0...  8.09 us
  transfers between devices with their start and end apart: 9, of which 5 were waited for; matrix products, arithmetic and copies ran while one was open for 25% of the time, Pallas kernels for 0%

profile of v2, /device:TPU:30, one launch (start us, length us, event | category | flops | bytes accessed | tf_op | source)
XLA Modules:
  0.0 240.1 jit_solution(13536726533344195686)
XLA Ops:
  6.5 0.7 all-gather.7.cloned.1.call-update
  7.3 0.7 all-gather.9.cloned.1.call-update
  8.1 0.7 all-gather.11.cloned.1.call-update
  11.2 2.0 convolution_convert_fusion.5
  13.1 8.5 %all-to-all-start = ((bf16[8,32,3584]{2,1,0:T(8,128)(2,1)}), bf16[8,32,3584]{2,1,0:T(8,128)(2,1)S(1)}, u32[]{:S(2)}, u32[]{:S(2)}) async-start(bf16[8,32,3584]{2,1,0:T(8,128)(2,1)} %bitcast.4), calls=%async_computation | async-start | bytes 3670016 | tf_op jit(solution)/shard_map/all_to_all | solution.py:30
  21.6 2.0 convolution_convert_fusion.2
  23.6 43.6 %all-to-all-done = bf16[8,32,3584]{2,1,0:T(8,128)(2,1)S(1)} async-done(((bf16[8,32,3584]{2,1,0:T(8,128)(2,1)}), bf16[8,32,3584]{2,1,0:T(8,128)(2,1)S(1)}, u32[]{:S(2)}, u32[]{:S(2)}) %all-to-all-start) | async-done | bytes 1835040 | tf_op jit(solution)/shard_map/all_to_all | solution.py:30
  67.2 1.2 copy-done.5
  68.4 3.6 %all-to-all-start.2 = ((bf16[8,32,3584]{2,1,0:T(8,128)(2,1)}), bf16[8,32,3584]{2,1,0:T(8,128)(2,1)S(1)}, u32[]{:S(2)}, u32[]{:S(2)}) async-start(bf16[8,32,3584]{2,1,0:T(8,128)(2,1)} %bitcast.21), calls=%async_computation.2 | async-start | bytes 3670016 | tf_op jit(solution)/shard_map/all_to_all | solution.py:30
  72.0 10.4 %copy.38 = bf16[2,1,3584,512]{2,3,0,1:T(8,128)(2,1)} copy(bf16[2,1,3584,512]{3,2,1,0:T(8,128)(2,1)} %all-gather.7.cloned.1.call-done) | data formatting | bytes 14680064 | tf_op jit(solution)/shard_map/all_gather | solution.py:40
  82.4 10.2 %copy.39 = bf16[2,1,3584,512]{2,3,0,1:T(8,128)(2,1)} copy(bf16[2,1,3584,512]{3,2,1,0:T(8,128)(2,1)} %all-gather.9.cloned.1.call-done) | data formatting | bytes 14680064 | tf_op jit(solution)/shard_map/all_gather | solution.py:41
  92.6 5.9 %fusion.37 = f32[256,1024]{1,0:T(8,128)S(1)} fusion(bf16[256,3584]{1,0:T(8,128)(2,1)} %bitcast.81, bf16[3584,1024]{0,1:T(8,128)(2,1)} %bitcast.74), kind=kOutput, calls=%fused_computation.68 | convolution fusion | flops 1879048192 | bytes 10223616 | tf_op jit(solution)/shard_map/dot_general | solution.py:16
  98.5 0.3 copy-done.6
  98.8 2.1 fusion.10
  101.0 3.3 %fusion.7 = f32[256,3584]{1,0:T(8,128)S(1)} fusion(bf16[2,1,512,3584]{3,2,1,0:T(8,128)(2,1)} %all-gather.11.cloned.1.call-done, bf16[256,1024]{1,0:T(8,128)(2,1)S(1)} %fusion.10), kind=kOutput, calls=%fused_computation.12 | convolution fusion | flops 941359104 | bytes 7602176 | tf_op jit(solution)/shard_map/dot_general | solution.py:20
  104.3 0.9 copy-done
  105.2 2.4 %fusion.6 = bf16[256,3584]{1,0:T(8,128)(2,1)} fusion(f32[256,3584]{1,0:T(8,128)S(1)} %fusion.7, bf16[2,1,512,3584]{3,2,1,0:T(8,128)(2,1)S(1)} %copy-done, bf16[256,1024]{1,0:T(8,128)(2,1)S(1)} %fusion.10), kind=kOutput, calls=%fused_computation.10 | convolution fusion | flops 943194112 | bytes 9437184 | tf_op jit(solution)/shard_map/dot_general | solution.py:21
  107.6 10.4 %all-to-all-done.2 = bf16[8,32,3584]{2,1,0:T(8,128)(2,1)S(1)} async-done(((bf16[8,32,3584]{2,1,0:T(8,128)(2,1)}), bf16[8,32,3584]{2,1,0:T(8,128)(2,1)S(1)}, u32[]{:S(2)}, u32[]{:S(2)}) %all-to-all-start.2) | async-done | bytes 1835040 | tf_op jit(solution)/shard_map/all_to_all | solution.py:30
  118.0 1.2 copy-done.3
  119.2 3.8 %all-to-all-start.1 = ((bf16[8,32,3584]{2,1,0:T(8,128)(2,1)}), bf16[8,32,3584]{2,1,0:T(8,128)(2,1)S(1)}, u32[]{:S(2)}, u32[]{:S(2)}) async-start(bf16[8,32,3584]{2,1,0:T(8,128)(2,1)} %bitcast.14), calls=%async_computation.1 | async-start | bytes 3670016 | tf_op jit(solution)/shard_map/all_to_all | solution.py:32
  123.0 5.9 %fusion.38 = f32[256,1024]{1,0:T(8,128)S(1)} fusion(bf16[256,3584]{1,0:T(8,128)(2,1)} %bitcast.79, bf16[3584,1024]{0,1:T(8,128)(2,1)} %bitcast.75), kind=kOutput, calls=%fused_computation.69 | convolution fusion | flops 1879048192 | bytes 10223616 | tf_op jit(solution)/shard_map/dot_general | solution.py:16
  128.9 5.4 %fusion.11 = bf16[256,1024]{1,0:T(8,128)(2,1)S(1)} fusion(bf16[256,3584]{1,0:T(8,128)(2,1)S(1)} %bitcast.80, bf16[3584,1024]{0,1:T(8,128)(2,1)} %bitcast.76, f32[256,1024]{1,0:T(8,128)S(1)} %fusion.38), kind=kOutput, calls=%fused_computation.27 | convolution fusion | flops 1880621056 | bytes 10747904 | tf_op jit(solution)/shard_map/dot_general | solution.py:17
  134.3 1.1 fusion.3
  135.5 2.4 %fusion.2 = bf16[256,3584]{1,0:T(8,128)(2,1)} fusion(f32[256,3584]{1,0:T(8,128)S(1)} %fusion.3, bf16[2,1,512,3584]{3,2,1,0:T(8,128)(2,1)S(1)} %bitcast.73, bf16[256,1024]{1,0:T(8,128)(2,1)S(1)} %fusion.11), kind=kOutput, calls=%fused_computation.3 | convolution fusion | flops 943194112 | bytes 9437184 | tf_op jit(solution)/shard_map/dot_general | solution.py:21
  137.9 28.7 %all-to-all-done.1 = bf16[8,32,3584]{2,1,0:T(8,128)(2,1)S(1)} async-done(((bf16[8,32,3584]{2,1,0:T(8,128)(2,1)}), bf16[8,32,3584]{2,1,0:T(8,128)(2,1)S(1)}, u32[]{:S(2)}, u32[]{:S(2)}) %all-to-all-start.1) | async-done | bytes 1835040 | tf_op jit(solution)/shard_map/all_to_all | solution.py:32
  166.6 4.3 %all-to-all-start.3 = ((bf16[8,32,3584]{2,1,0:T(8,128)(2,1)}), bf16[8,32,3584]{2,1,0:T(8,128)(2,1)}, u32[]{:S(2)}, u32[]{:S(2)}) async-start(bf16[8,32,3584]{2,1,0:T(8,128)(2,1)} %bitcast.27), calls=%async_computation.3 | async-start | bytes 3670016 | tf_op jit(solution)/shard_map/all_to_all | solution.py:32
  171.0 1.1 fusion.8
  172.2 44.8 %all-to-all-done.3 = bf16[8,32,3584]{2,1,0:T(8,128)(2,1)} async-done(((bf16[8,32,3584]{2,1,0:T(8,128)(2,1)}), bf16[8,32,3584]{2,1,0:T(8,128)(2,1)}, u32[]{:S(2)}, u32[]{:S(2)}) %all-to-all-start.3) | async-done | bytes 1835040 | tf_op jit(solution)/shard_map/all_to_all | solution.py:32
  217.0 2.6 %fusion.9 = bf16[64,3584]{1,0:T(8,128)(2,1)S(1)} fusion(f32[256,64]{0,1:T(8,128)S(1)} %get-tuple-element.10, bf16[256,3584]{1,0:T(8,128)(2,1)} %bitcast.28, bf16[1,2,64,3584]{3,2,1,0:T(8,128)(2,1)S(1)} %copy-done.1), kind=kOutput, calls=%fused_computation.17 | convolution fusion | flops 705331200 | bytes 2818048 | tf_op jit(solution)/shard_map/dot_general | solution.py:77
  219.6 0.9 collective-permute-start.1
  220.5 12.0 %collective-permute-done.1 = bf16[64,3584]{1,0:T(8,128)(2,1)S(1)} collective-permute-done((bf16[64,3584]{1,0:T(8,128)(2,1)S(1)}, bf16[64,3584]{1,0:T(8,128)(2,1)S(1)}, u32[]{:S(2)}, u32[]{:S(2)}) %collective-permute-start.1) | collective-permute-done | bytes 458784 | tf_op jit(solution)/shard_map/ppermute | solution.py:12
  232.5 1.0 maximum_bitcast_fusion
  (50 shorter events, 2.6 us)
Async XLA Ops:
  6.5 65.5 %all-gather.7.cloned.1.call-start = ((), (), s32[]{:S(2)}) async-start(), calls=%async_computation.4 | async-start | bytes 11010048 | tf_op jit(solution)/shard_map/all_gather | solution.py:40
  7.3 1.5 copy-start.8
  7.3 3.4 %copy-start.7 = (f32[1,3584]{1,0:T(1,128)S(1)}, f32[1,3584]{1,0:T(1,128)}, u32[]{:S(2)}) copy-start(f32[1,3584]{1,0:T(1,128)} %param.8) | copy-start | bytes 43012
  7.3 3.4 %copy-start.9 = (f32[1,2,64,2]{2,3,1,0:T(2,128)S(1)}, f32[1,2,64,2]{2,3,1,0:T(2,128)}, u32[]{:S(2)}) copy-start(f32[1,2,64,2]{2,3,1,0:T(2,128)} %param.13) | copy-start | bytes 3076
  7.3 3.6 %copy-start.1 = (bf16[1,2,64,3584]{3,2,1,0:T(8,128)(2,1)S(1)}, bf16[1,2,64,3584]{3,2,1,0:T(8,128)(2,1)}, u32[]{:S(2)}) copy-start(bf16[1,2,64,3584]{3,2,1,0:T(8,128)(2,1)} %param.7) | copy-start | bytes 2752516
  7.3 75.1 %all-gather.9.cloned.1.call-start = ((), (), s32[]{:S(2)}) async-start(), calls=%async_computation.5 | async-start | bytes 11010048 | tf_op jit(solution)/shard_map/all_gather | solution.py:41
  8.0 92.9 %all-gather.11.cloned.1.call-start = ((), (), s32[]{:S(2)}) async-start(), calls=%async_computation.6 | async-start | bytes 11010048 | tf_op jit(solution)/shard_map/all_gather | solution.py:42
  13.1 54.0 %all-to-all-start = ((bf16[8,32,3584]{2,1,0:T(8,128)(2,1)}), bf16[8,32,3584]{2,1,0:T(8,128)(2,1)S(1)}, u32[]{:S(2)}, u32[]{:S(2)}) async-start(bf16[8,32,3584]{2,1,0:T(8,128)(2,1)} %bitcast.4), calls=%async_computation | async-start | bytes 3670016 | tf_op jit(solution)/shard_map/all_to_all | solution.py:30
  67.2 1.2 copy-start.5
  68.4 49.6 %all-to-all-start.2 = ((bf16[8,32,3584]{2,1,0:T(8,128)(2,1)}), bf16[8,32,3584]{2,1,0:T(8,128)(2,1)S(1)}, u32[]{:S(2)}, u32[]{:S(2)}) async-start(bf16[8,32,3584]{2,1,0:T(8,128)(2,1)} %bitcast.21), calls=%async_computation.2 | async-start | bytes 3670016 | tf_op jit(solution)/shard_map/all_to_all | solution.py:30
  92.6 5.9 %copy-start.2 = (bf16[2,1,3584,512]{2,3,0,1:T(8,128)(2,1)S(1)}, bf16[2,1,3584,512]{2,3,0,1:T(8,128)(2,1)}, u32[]{:S(2)}) copy-start(bf16[2,1,3584,512]{2,3,0,1:T(8,128)(2,1)} %copy.39) | copy-start | bytes 22020100
  92.6 6.2 %copy-start.6 = (bf16[8,32,3584]{2,1,0:T(8,128)(2,1)S(1)}, bf16[8,32,3584]{2,1,0:T(8,128)(2,1)}, u32[]{:S(2)}) copy-start(bf16[8,32,3584]{2,1,0:T(8,128)(2,1)} %copy-done.5) | copy-start | bytes 5505028
  101.0 4.2 %copy-start = (bf16[2,1,512,3584]{3,2,1,0:T(8,128)(2,1)S(1)}, bf16[2,1,512,3584]{3,2,1,0:T(8,128)(2,1)}, u32[]{:S(2)}) copy-start(bf16[2,1,512,3584]{3,2,1,0:T(8,128)(2,1)} %all-gather.11.cloned.1.call-done) | copy-start | bytes 22020100
  118.0 1.2 copy-start.3
  119.2 47.4 %all-to-all-start.1 = ((bf16[8,32,3584]{2,1,0:T(8,128)(2,1)}), bf16[8,32,3584]{2,1,0:T(8,128)(2,1)S(1)}, u32[]{:S(2)}, u32[]{:S(2)}) async-start(bf16[8,32,3584]{2,1,0:T(8,128)(2,1)} %bitcast.14), calls=%async_computation.1 | async-start | bytes 3670016 | tf_op jit(solution)/shard_map/all_to_all | solution.py:32
  123.0 5.9 %copy-start.4 = (bf16[8,32,3584]{2,1,0:T(8,128)(2,1)S(1)}, bf16[8,32,3584]{2,1,0:T(8,128)(2,1)}, u32[]{:S(2)}) copy-start(bf16[8,32,3584]{2,1,0:T(8,128)(2,1)} %copy-done.3) | copy-start | bytes 5505028
  123.0 11.3 %slice-start = ((s8[7340032]{0:T(1024)(128)(4,1)}), s8[4194304]{0:T(1024)(128)(4,1)S(1)}, s32[]{:S(2)}) async-start(s8[7340032]{0:T(1024)(128)(4,1)} %bitcast.72), calls=%async_computation.7 | async-start | bytes 8388608
  128.9 5.4 %slice-start.1 = ((s8[7340032]{0:T(1024)(128)(4,1)}), s8[3145728]{0:T(1024)(128)(4,1)S(1)}, s32[]{:S(2)}) async-start(s8[7340032]{0:T(1024)(128)(4,1)} %bitcast.72), calls=%async_computation.8 | async-start | bytes 6291456
  166.6 50.4 %all-to-all-start.3 = ((bf16[8,32,3584]{2,1,0:T(8,128)(2,1)}), bf16[8,32,3584]{2,1,0:T(8,128)(2,1)}, u32[]{:S(2)}, u32[]{:S(2)}) async-start(bf16[8,32,3584]{2,1,0:T(8,128)(2,1)} %bitcast.27), calls=%async_computation.3 | async-start | bytes 3670016 | tf_op jit(solution)/shard_map/all_to_all | solution.py:32
  172.0 48.4 %collective-permute-start = (bf16[64,3584]{1,0:T(8,128)(2,1)S(1)}, bf16[64,3584]{1,0:T(8,128)(2,1)S(1)}, u32[]{:S(2)}, u32[]{:S(2)}) collective-permute-start(bf16[64,3584]{1,0:T(8,128)(2,1)S(1)} %fusion.8), channel_id=1, source_target_pairs={{0,16},{16,32},{32,48},{48,64},{64,80},{80,96},{96,112},{112,128},... | collective-permute-start | bytes 1376264 | tf_op jit(solution)/shard_map/ppermute | solution.py:12
  219.6 13.0 %collective-permute-start.1 = (bf16[64,3584]{1,0:T(8,128)(2,1)S(1)}, bf16[64,3584]{1,0:T(8,128)(2,1)S(1)}, u32[]{:S(2)}, u32[]{:S(2)}) collective-permute-start(bf16[64,3584]{1,0:T(8,128)(2,1)S(1)} %fusion.9), channel_id=1, source_target_pairs={{0,240},{16,0},{32,16},{48,32},{64,48},{80,64},{96,80},{112,96},{1... | collective-permute-start | bytes 1376264 | tf_op jit(solution)/shard_map/ppermute | solution.py:12
Sparse Core Ops, SparseCore 0:
  9.1 26.2 all-gather.6
  37.2 24.9 all-gather.8
  64.0 24.9 all-gather.10

commit v3 on v2

v3 whole, which is shorter than its diff:
```python
import functools

import jax
import jax.numpy as jnp
import numpy as np
from jax import lax
from jax.experimental import pallas as pl
from jax.experimental.pallas import tpu as pltpu
from jax.sharding import Mesh
from jax.sharding import PartitionSpec as P


def from_behind(value, axis, steps):
    count = lax.axis_size(axis)
    pairs = [(source, (source + steps) % count) for source in range(count)]
    return lax.ppermute(value, axis, pairs)


MESH = pl.DeviceIdType.MESH


def moe_kernel(
    chips, xs_hbm, wg_hbm, wu_hbm, wd_hbm, ys_hbm,
    recv, res, wg, wu, wd, dsend, drecv, rsend, rrecv, lsem, wsem,
):
    streams, rows, width = recv.shape
    cap = rows // chips
    pipe = lax.axis_index("pipe")
    me = lax.axis_index("ez")
    core = lax.axis_index("ec")

    def dev(p):
        return (pipe, p, core)

    def blk(p):
        return pl.ds(pl.multiple_of(p * cap, cap), cap)

    weight_copies = [
        pltpu.make_async_copy(wg_hbm, wg, wsem.at[0]),
        pltpu.make_async_copy(wu_hbm, wu, wsem.at[1]),
        pltpu.make_async_copy(wd_hbm, wd, wsem.at[2]),
    ]
    for c in weight_copies:
        c.start()

    barrier = pltpu.get_barrier_semaphore()
    for k in range(1, chips):
        pl.semaphore_signal(
            barrier, inc=1, device_id=dev(lax.rem(me + k, chips)), device_id_type=MESH
        )
    pl.semaphore_wait(barrier, chips - 1)

    def dispatch(s, k):
        p = lax.rem(me + k, chips)
        return pltpu.make_async_remote_copy(
            src_ref=xs_hbm.at[s, blk(p)], dst_ref=recv.at[s, blk(me)],
            send_sem=dsend.at[s, k], recv_sem=drecv.at[s, me],
            device_id=dev(p), device_id_type=MESH,
        )

    def dispatch_in(s, k):
        q = lax.rem(me + chips - k, chips)
        return pltpu.make_async_remote_copy(
            src_ref=xs_hbm.at[s, blk(q)], dst_ref=recv.at[s, blk(q)],
            send_sem=dsend.at[s, k], recv_sem=drecv.at[s, q],
            device_id=dev(q), device_id_type=MESH,
        )

    def back(s, k):
        p = lax.rem(me + k, chips)
        return pltpu.make_async_remote_copy(
            src_ref=res.at[s, blk(p)], dst_ref=ys_hbm.at[s, blk(me)],
            send_sem=rsend.at[s, k], recv_sem=rrecv.at[s, me],
            device_id=dev(p), device_id_type=MESH,
        )

    def back_in(s, k):
        q = lax.rem(me + chips - k, chips)
        return pltpu.make_async_remote_copy(
            src_ref=res.at[s, blk(q)], dst_ref=ys_hbm.at[s, blk(q)],
            send_sem=rsend.at[s, k], recv_sem=rrecv.at[s, q],
            device_id=dev(q), device_id_type=MESH,
        )

    local_in = [
        pltpu.make_async_copy(xs_hbm.at[s, blk(me)], recv.at[s, blk(me)], lsem.at[0, s])
        for s in range(streams)
    ]
    local_out = [
        pltpu.make_async_copy(res.at[s, blk(me)], ys_hbm.at[s, blk(me)], lsem.at[1, s])
        for s in range(streams)
    ]
    for s in range(streams):
        local_in[s].start()
        for k in range(1, chips):
            dispatch(s, k).start()
    for c in weight_copies:
        c.wait()

    tile = 128
    for s in range(streams):
        local_in[s].wait()
        for k in range(1, chips):
            dispatch_in(s, k).wait_recv()
        for b in range(rows // tile):
            x = recv[s, pl.ds(b * tile, tile), :]
            total = None
            for j in range(2):
                gate_val = jnp.dot(x, wg[j], preferred_element_type=jnp.float32)
                up_val = jnp.dot(x, wu[j], preferred_element_type=jnp.float32)
                hidden = (jax.nn.silu(gate_val) * up_val).astype(jnp.bfloat16)
                part = jnp.dot(hidden, wd[j], preferred_element_type=jnp.float32)
                part = part.astype(jnp.bfloat16).astype(jnp.float32)
                total = part if total is None else total + part
            res[s, pl.ds(b * tile, tile), :] = total.astype(jnp.bfloat16)
        local_out[s].start()
        for k in range(1, chips):
            back(s, k).start()

    for s in range(streams):
        for k in range(1, chips):
            dispatch(s, k).wait_send()
    for s in range(streams):
        local_out[s].wait()
        for k in range(1, chips):
            back(s, k).wait_send()
        for k in range(1, chips):
            back_in(s, k).wait_recv()


def expert_pass(outgoing, gate_pair, up_pair, down_pair):
    streams, rows, width = outgoing.shape
    chips = lax.axis_size("ez")
    hbm = pl.BlockSpec(memory_space=pl.ANY)
    return pl.pallas_call(
        functools.partial(moe_kernel, chips),
        out_shape=jax.ShapeDtypeStruct(outgoing.shape, jnp.bfloat16),
        in_specs=[hbm] * 4,
        out_specs=hbm,
        scratch_shapes=[
            pltpu.VMEM(outgoing.shape, jnp.bfloat16),
            pltpu.VMEM(outgoing.shape, jnp.bfloat16),
            pltpu.VMEM(gate_pair.shape, jnp.bfloat16),
            pltpu.VMEM(up_pair.shape, jnp.bfloat16),
            pltpu.VMEM(down_pair.shape, jnp.bfloat16),
            pltpu.SemaphoreType.DMA((streams, chips)),
            pltpu.SemaphoreType.DMA((streams, chips)),
            pltpu.SemaphoreType.DMA((streams, chips)),
            pltpu.SemaphoreType.DMA((streams, chips)),
            pltpu.SemaphoreType.DMA((2, streams)),
            pltpu.SemaphoreType.DMA((3,)),
        ],
        compiler_params=pltpu.CompilerParams(
            collective_id=0, has_side_effects=True, vmem_limit_bytes=62 * 1024 * 1024
        ),
    )(outgoing, gate_pair, up_pair, down_pair)


def body(streams, norm_gain, w_gate, w_up, w_down, routes, gate_weights):
    experts = lax.axis_size("ez")
    gate_pair = lax.all_gather(w_gate[0, 0], "ec")
    up_pair = lax.all_gather(w_up[0, 0], "ec")
    down_pair = lax.all_gather(w_down[0, 0], "ec")
    gain_row = norm_gain[0]
    tok_rows = streams.shape[2]
    width = streams.shape[3]
    top_count = routes.shape[3]
    capacity = 2 * tok_rows * top_count // experts
    lane_count = experts * capacity
    lane_index = jnp.arange(lane_count, dtype=jnp.int32)
    expert_index = jnp.arange(experts, dtype=jnp.int32)
    states, outgoings, combines = [], [], []
    for stream in range(2):
        state = streams[0, stream].astype(jnp.float32)
        normed = (
            state * lax.rsqrt(jnp.mean(state * state, axis=-1, keepdims=True) + 1e-06) * gain_row
        ).astype(jnp.bfloat16)
        chosen = routes[0, stream].reshape(-1)
        onehot = (chosen[:, None] == expert_index[None, :]).astype(jnp.int32)
        slot_rank = jnp.sum((jnp.cumsum(onehot, axis=0) - onehot) * onehot, axis=1)
        lane_of = chosen * capacity + slot_rank
        matches = lane_index[:, None] == lane_of[None, :]
        send_matrix = jnp.sum(
            matches.reshape(lane_count, tok_rows, top_count).astype(jnp.float32), axis=-1
        ).astype(jnp.bfloat16)
        outgoing = jnp.dot(send_matrix, normed, preferred_element_type=jnp.float32).astype(
            jnp.bfloat16
        )
        weights = gate_weights[0, stream].reshape(-1)
        combine = jnp.sum(
            (matches.astype(jnp.float32) * weights[None, :]).reshape(
                lane_count, tok_rows, top_count
            ),
            axis=-1,
        ).T
        states.append(state)
        outgoings.append(outgoing)
        combines.append(combine)
    expert_rows = expert_pass(jnp.stack(outgoings), gate_pair, up_pair, down_pair)
    results = []
    for stream in range(2):
        mixed = states[stream] + jnp.dot(
            combines[stream],
            expert_rows[stream].astype(jnp.float32),
            precision=lax.Precision.HIGHEST,
            preferred_element_type=jnp.float32,
        )
        results.append(mixed.astype(jnp.bfloat16))
    forward = from_behind(results[0], "pipe", 1)
    backward = from_behind(results[1], "pipe", -1)
    return jnp.stack([forward, backward])[None]


def solution(mesh):
    pipe_size, expert_size = mesh.devices.shape
    split = Mesh(
        np.asarray(mesh.devices).reshape(pipe_size, expert_size // 2, 2), ("pipe", "ez", "ec")
    )
    tok = ("ez", "ec")
    return jax.shard_map(
        body,
        mesh=split,
        in_specs=(
            P("pipe", None, tok, None),
            P("pipe", None),
            P("pipe", tok, None, None),
            P("pipe", tok, None, None),
            P("pipe", tok, None, None),
            P("pipe", None, tok, None),
            P("pipe", None, tok, None),
        ),
        out_specs=P("pipe", None, tok, None),
        check_vma=False,
    )
```

time: 242 us -> 283 us (1.17)
  Pallas kernels: 0 us -> 166 us
  waiting for transfers between devices: 142 us -> 90 us
  matrix products: 36.1 us -> 6.51 us
  local copies, waits for them, and re-layouts: 25.2 us -> 0.91 us
  starting transfers between devices: 21.3 us -> 2.18 us
    pallas_call x0 -> x1, Pallas kernels: none -> 166 us  [expert_pass(): pl.pallas_call(functools.partial(moe_kernel, chips), out_shape=jax.ShapeD...]
    all_to_all x4 -> x0, waiting for transfers between devices: 127 us -> none  [the longest x2 73.5 us: expert_pass(): lax.all_to_all(summed.reshape(chips, capacity, width), 'ez', split_axis=0...]
    all_gather x2, waiting for transfers between devices: 0.02 us -> 47.5 us  [the longest x1 26.8 us: body(): up_pair = lax.all_gather(w_up[0, 0], 'ec')]
    dot_general x10 -> x2, matrix products: 32.2 us -> 5.12 us  [body(): jnp.dot(combines[stream], expert_rows[stream].astype(jnp.float32), precis...]
    all_gather x1, waiting for transfers between devices: 0.02 us -> 26.8 us  [body(): down_pair = lax.all_gather(w_down[0, 0], 'ec')]
    all_gather x2 -> x0, local copies, waits for them, and re-layouts: 20.5 us -> none  [the longest x1 10.4 us: body(): gate_full = jnp.concatenate(lax.all_gather(w_gate[0, 0], 'ec'), axis=1)]
    all_to_all x4 -> x0, starting transfers between devices: 20.2 us -> none  [the longest x2 12.1 us: expert_pass(): lax.all_to_all(outgoing, 'ez', split_axis=0, concat_axis=0, tiled=True)]
    unnamed x24 -> x8, local copies, waits for them, and re-layouts: 3.74 us -> 0.02 us
  transfers between devices with their start and end apart: 9 -> 5, of which waited for: 5 -> 5; matrix products, arithmetic and copies ran while one was open for 25% -> 2% of each run, Pallas kernels for 0% -> 0%
where the time goes in v3:
time: 283 us
  Pallas kernels  166 us (59%)
  waiting for transfers between devices  90 us (32%)
  between operations  13.3 us (5%)
  matrix products  6.51 us (2%)
  other arithmetic  4.54 us (2%)
    pallas_call x1, Pallas kernels, expert_pass(): pl.pallas_call(functools.partial(moe_kernel, chips), out_shape=jax.ShapeD...  166 us
    all_gather x1, waiting for transfers between devices, body(): down_pair = lax.all_gather(w_down[0, 0], 'ec')  26.8 us
    all_gather x1, waiting for transfers between devices, body(): up_pair = lax.all_gather(w_up[0, 0], 'ec')  26.8 us
    all_gather x1, waiting for transfers between devices, body(): gate_pair = lax.all_gather(w_gate[0, 0], 'ec')  20.7 us
    ppermute x2, waiting for transfers between devices, from_behind(): return lax.ppermute(value, axis, pairs)  13.7 us
  transfers between devices with their start and end apart: 5, of which 5 were waited for; matrix products, arithmetic and copies ran while one was open for 2% of the time, Pallas kernels for 0%

profile of v3, /device:TPU:30, one launch (start us, length us, event | category | flops | bytes accessed | tf_op | source)
XLA Modules:
  0.0 283.1 jit_solution(12189971905700493357)
XLA Ops:
  6.5 0.7 all-gather.7.cloned.1.call-update
  7.3 0.7 all-gather.9.cloned.1.call-update
  8.1 0.7 all-gather.11.cloned.1.call-update
  8.8 0.1 copy.38
  8.9 0.1 eq.61
  9.0 0.1 copy.40
  9.1 0.1 eq.68
  9.3 0.1 fusion.24
  9.4 0.2 reduce_window_sum.18
  9.5 0.2 select_reduce_fusion.2
  9.7 0.1 reduce_sum.82
  9.9 0.1 copy.41
  9.9 0.1 fusion.25
  10.0 0.2 reduce_window_sum.17
  10.2 0.2 select_reduce_fusion.3
  10.4 0.1 reduce_sum.77
  10.7 0.1 convert_reduce_fusion
  10.9 0.3 fusion.8
  11.2 0.7 fusion.1
  11.9 0.7 fusion
  12.6 2.2 pad_maximum_fusion.xs_hbm
  14.7 20.7 %all-gather.7.cloned.1.call-done = bf16[2,1,3584,512]{3,2,1,0:T(8,128)(2,1)} async-done(((bf16[1,1,3584,512]{3,2,1,0:T(8,128)(2,1)}), bf16[2,1,3584,512]{3,2,1,0:T(8,128)(2,1)}) %all-gather.7.cloned.1.call-update) | async-done | bytes 7340048 | tf_op jit(solution)/shard_map/all_gather | solution.py:161
  35.5 26.8 %all-gather.9.cloned.1.call-done = bf16[2,1,3584,512]{3,2,1,0:T(8,128)(2,1)} async-done(((bf16[1,1,3584,512]{3,2,1,0:T(8,128)(2,1)}), bf16[2,1,3584,512]{3,2,1,0:T(8,128)(2,1)}) %all-gather.9.cloned.1.call-update) | async-done | bytes 7340048 | tf_op jit(solution)/shard_map/all_gather | solution.py:162
  62.2 26.8 %all-gather.11.cloned.1.call-done = bf16[2,1,512,3584]{3,2,1,0:T(8,128)(2,1)} async-done(((bf16[1,1,512,3584]{3,2,1,0:T(8,128)(2,1)}), bf16[2,1,512,3584]{3,2,1,0:T(8,128)(2,1)}) %all-gather.11.cloned.1.call-update) | async-done | bytes 7340048 | tf_op jit(solution)/shard_map/all_gather | solution.py:163
  89.0 165.7 %shard_map.73 = bf16[2,256,3584]{2,1,0:T(8,128)(2,1)} custom-call(bf16[2,256,3584]{2,1,0:T(8,128)(2,1)} %pad_maximum_fusion.xs_hbm, bf16[2,3584,512]{2,1,0:T(8,128)(2,1)} %bitcast.49, bf16[2,3584,512]{2,1,0:T(8,128)(2,1)} %bitcast.50, bf16[2,512,3584]{2,1,0:T(8,128)(2,1)} %bitcast.51), custom_call_target="tpu_custom_call" | custom-call | tf_op jit(solution)/shard_map/pallas_call | solution.py:135
  254.7 2.6 fusion.3
  257.2 2.6 fusion.2
  259.8 0.5 collective-permute-start
  260.3 1.6 collective-permute-start.1
  261.9 10.2 %collective-permute-done = bf16[64,3584]{1,0:T(8,128)(2,1)S(1)} collective-permute-done((bf16[64,3584]{1,0:T(8,128)(2,1)S(1)}, bf16[64,3584]{1,0:T(8,128)(2,1)S(1)}, u32[]{:S(2)}, u32[]{:S(2)}) %collective-permute-start) | collective-permute-done | bytes 458784 | tf_op jit(solution)/shard_map/ppermute | solution.py:16
  272.1 3.5 %collective-permute-done.1 = bf16[64,3584]{1,0:T(8,128)(2,1)S(1)} collective-permute-done((bf16[64,3584]{1,0:T(8,128)(2,1)S(1)}, bf16[64,3584]{1,0:T(8,128)(2,1)S(1)}, u32[]{:S(2)}, u32[]{:S(2)}) %collective-permute-start.1) | collective-permute-done | bytes 458784 | tf_op jit(solution)/shard_map/ppermute | solution.py:16
  275.6 1.0 maximum_bitcast_fusion
  (17 shorter events, 0.2 us)
Async XLA Ops:
  6.5 28.9 %all-gather.7.cloned.1.call-start = ((), (), s32[]{:S(2)}) async-start(), calls=%async_computation | async-start | bytes 11010048 | tf_op jit(solution)/shard_map/all_gather | solution.py:161
  7.3 1.5 copy-start.2
  7.3 3.4 %copy-start.1 = (f32[1,3584]{1,0:T(1,128)S(1)}, f32[1,3584]{1,0:T(1,128)}, u32[]{:S(2)}) copy-start(f32[1,3584]{1,0:T(1,128)} %param.8) | copy-start | bytes 43012
  7.3 3.4 %copy-start.3 = (f32[1,2,64,2]{2,3,1,0:T(2,128)S(1)}, f32[1,2,64,2]{2,3,1,0:T(2,128)}, u32[]{:S(2)}) copy-start(f32[1,2,64,2]{2,3,1,0:T(2,128)} %param.13) | copy-start | bytes 3076
  7.3 3.6 %copy-start = (bf16[1,2,64,3584]{3,2,1,0:T(8,128)(2,1)S(1)}, bf16[1,2,64,3584]{3,2,1,0:T(8,128)(2,1)}, u32[]{:S(2)}) copy-start(bf16[1,2,64,3584]{3,2,1,0:T(8,128)(2,1)} %param.7) | copy-start | bytes 2752516
  7.3 54.9 %all-gather.9.cloned.1.call-start = ((), (), s32[]{:S(2)}) async-start(), calls=%async_computation.1 | async-start | bytes 11010048 | tf_op jit(solution)/shard_map/all_gather | solution.py:162
  8.0 80.9 %all-gather.11.cloned.1.call-start = ((), (), s32[]{:S(2)}) async-start(), calls=%async_computation.2 | async-start | bytes 11010048 | tf_op jit(solution)/shard_map/all_gather | solution.py:163
  259.8 12.3 %collective-permute-start = (bf16[64,3584]{1,0:T(8,128)(2,1)S(1)}, bf16[64,3584]{1,0:T(8,128)(2,1)S(1)}, u32[]{:S(2)}, u32[]{:S(2)}) collective-permute-start(bf16[64,3584]{1,0:T(8,128)(2,1)S(1)} %fusion.2), channel_id=1, source_target_pairs={{0,16},{16,32},{32,48},{48,64},{64,80},{80,96},{96,112},{112,128},... | collective-permute-start | bytes 1376264 | tf_op jit(solution)/shard_map/ppermute | solution.py:16
  260.3 15.3 %collective-permute-start.1 = (bf16[64,3584]{1,0:T(8,128)(2,1)S(1)}, bf16[64,3584]{1,0:T(8,128)(2,1)S(1)}, u32[]{:S(2)}, u32[]{:S(2)}) collective-permute-start(bf16[64,3584]{1,0:T(8,128)(2,1)S(1)} %fusion.3), channel_id=1, source_target_pairs={{0,240},{16,0},{32,16},{48,32},{64,48},{80,64},{96,80},{112,96},{1... | collective-permute-start | bytes 1376264 | tf_op jit(solution)/shard_map/ppermute | solution.py:16
Sparse Core Ops, SparseCore 0:
  9.2 26.2 all-gather.6
  37.3 24.9 all-gather.8
  64.0 24.9 all-gather.10

commit v4 on v3

--- a/solution.py
+++ b/solution.py
@@ -35,12 +35,13 @@
     def blk(p):
         return pl.ds(pl.multiple_of(p * cap, cap), cap)
 
-    weight_copies = [
-        pltpu.make_async_copy(wg_hbm, wg, wsem.at[0]),
-        pltpu.make_async_copy(wu_hbm, wu, wsem.at[1]),
-        pltpu.make_async_copy(wd_hbm, wd, wsem.at[2]),
-    ]
-    for c in weight_copies:
+    sibling = (pipe, me, 1 - core)
+    weights = ((wg_hbm, wg), (wu_hbm, wu), (wd_hbm, wd))
+    own_copies = [
+        pltpu.make_async_copy(src, dst.at[core], wsem.at[0, i])
+        for i, (src, dst) in enumerate(weights)
+    ]
+    for c in own_copies:
         c.start()
 
     barrier = pltpu.get_barrier_semaphore()
@@ -48,7 +49,23 @@
         pl.semaphore_signal(
             barrier, inc=1, device_id=dev(lax.rem(me + k, chips)), device_id_type=MESH
         )
-    pl.semaphore_wait(barrier, chips - 1)
+    pl.semaphore_signal(barrier, inc=1, device_id=sibling, device_id_type=MESH)
+    pl.semaphore_wait(barrier, chips)
+
+    to_sibling = [
+        pltpu.make_async_remote_copy(
+            src_ref=src, dst_ref=dst.at[core], send_sem=wsem.at[1, i], recv_sem=wsem.at[2, i],
+            device_id=sibling, device_id_type=MESH,
+        )
+        for i, (src, dst) in enumerate(weights)
+    ]
+    from_sibling = [
+        pltpu.make_async_remote_copy(
+            src_ref=src, dst_ref=dst.at[1 - core], send_sem=wsem.at[1, i],
+            recv_sem=wsem.at[2, i], device_id=sibling, device_id_type=MESH,
+        )
+        for i, (src, dst) in enumerate(weights)
+    ]
 
     def dispatch(s, k):
         p = lax.rem(me + k, chips)
@@ -94,8 +111,14 @@
         local_in[s].start()
         for k in range(1, chips):
             dispatch(s, k).start()
-    for c in weight_copies:
+    for c in to_sibling:
+        c.start()
+    for c in own_copies:
         c.wait()
+    for c in from_sibling:
+        c.wait_recv()
+    for c in to_sibling:
+        c.wait_send()
 
     tile = 128
     for s in range(streams):
@@ -128,7 +151,7 @@
             back_in(s, k).wait_recv()
 
 
-def expert_pass(outgoing, gate_pair, up_pair, down_pair):
+def expert_pass(outgoing, gate_half, up_half, down_half):
     streams, rows, width = outgoing.shape
     chips = lax.axis_size("ez")
     hbm = pl.BlockSpec(memory_space=pl.ANY)
@@ -140,27 +163,24 @@
         scratch_shapes=[
             pltpu.VMEM(outgoing.shape, jnp.bfloat16),
             pltpu.VMEM(outgoing.shape, jnp.bfloat16),
-            pltpu.VMEM(gate_pair.shape, jnp.bfloat16),
-            pltpu.VMEM(up_pair.shape, jnp.bfloat16),
-            pltpu.VMEM(down_pair.shape, jnp.bfloat16),
+            pltpu.VMEM((2,) + gate_half.shape, jnp.bfloat16),
+            pltpu.VMEM((2,) + up_half.shape, jnp.bfloat16),
+            pltpu.VMEM((2,) + down_half.shape, jnp.bfloat16),
             pltpu.SemaphoreType.DMA((streams, chips)),
             pltpu.SemaphoreType.DMA((streams, chips)),
             pltpu.SemaphoreType.DMA((streams, chips)),
             pltpu.SemaphoreType.DMA((streams, chips)),
             pltpu.SemaphoreType.DMA((2, streams)),
-            pltpu.SemaphoreType.DMA((3,)),
+            pltpu.SemaphoreType.DMA((3, 3)),
         ],
         compiler_params=pltpu.CompilerParams(
             collective_id=0, has_side_effects=True, vmem_limit_bytes=62 * 1024 * 1024
         ),
-    )(outgoing, gate_pair, up_pair, down_pair)
+    )(outgoing, gate_half, up_half, down_half)
 
 
 def body(streams, norm_gain, w_gate, w_up, w_down, routes, gate_weights):
     experts = lax.axis_size("ez")
-    gate_pair = lax.all_gather(w_gate[0, 0], "ec")
-    up_pair = lax.all_gather(w_up[0, 0], "ec")
-    down_pair = lax.all_gather(w_down[0, 0], "ec")
     gain_row = norm_gain[0]
     tok_rows = streams.shape[2]
     width = streams.shape[3]
@@ -196,7 +216,7 @@
         states.append(state)
         outgoings.append(outgoing)
         combines.append(combine)
-    expert_rows = expert_pass(jnp.stack(outgoings), gate_pair, up_pair, down_pair)
+    expert_rows = expert_pass(jnp.stack(outgoings), w_gate[0, 0], w_up[0, 0], w_down[0, 0])
     results = []
     for stream in range(2):
         mixed = states[stream] + jnp.dot(

time: 283 us -> 200 us (0.71)
  waiting for transfers between devices: 90 us -> 13.3 us
  between operations: 13.3 us -> 0.12 us
    all_gather x3 -> x0, waiting for transfers between devices: 74.2 us -> none  [the longest x1 26.8 us: body(): down_pair = lax.all_gather(w_down[0, 0], 'ec')]
  transfers between devices with their start and end apart: 5 -> 2, of which waited for: 5 -> 2; matrix products, arithmetic and copies ran while one was open for 2% -> 1% of each run, Pallas kernels for 0% -> 0%
where the time goes in v4:
time: 200 us; the launch traced here: 199 us
  Pallas kernels  167 us (84%)
  waiting for transfers between devices  13.3 us (7%)
  matrix products  7.51 us (4%)
  other arithmetic  7.12 us (4%)
  local copies, waits for them, and re-layouts  2.3 us (1%)
  starting transfers between devices  2.18 us (1%)
    pallas_call x1, Pallas kernels, expert_pass(): pl.pallas_call(functools.partial(moe_kernel, chips), out_shape=jax.ShapeD...  167 us
    ppermute x2, waiting for transfers between devices, from_behind(): return lax.ppermute(value, axis, pairs)  13.3 us
    dot_general x2, matrix products, body(): jnp.dot(combines[stream], expert_rows[stream].astype(jnp.float32), precis...  5.11 us
  transfers between devices with their start and end apart: 2, of which 2 were waited for; matrix products, arithmetic and copies ran while one was open for 1% of the time, Pallas kernels for 0%

profile of v4, /device:TPU:30, one launch (start us, length us, event | category | flops | bytes accessed | tf_op | source)
XLA Modules:
  0.0 199.5 jit_solution(11813761922257430611)
XLA Ops:
  0.0 1.5 fusion.8
  1.5 0.7 slice_bitcast_fusion.1
  2.2 0.7 fusion.28
  2.9 0.1 copy.24
  3.0 0.1 eq.61
  3.2 0.1 copy.26
  3.3 0.1 eq.68
  3.4 0.1 fusion.24
  3.5 0.2 reduce_window_sum.18
  3.7 0.2 select_reduce_fusion.2
  3.8 0.1 reduce_sum.82
  4.0 0.1 copy.27
  4.1 0.1 fusion.25
  4.2 0.2 reduce_window_sum.17
  4.3 0.2 select_reduce_fusion.3
  4.5 0.1 reduce_sum.77
  4.7 0.1 copy.25
  4.8 0.8 reduce
  5.5 0.7 bitcast_add_fusion.1
  6.2 0.1 convert_reduce_fusion
  6.4 1.7 fusion.1
  8.1 0.0 copy-done
  8.1 0.7 fusion
  8.8 2.1 %pad_maximum_fusion.xs_hbm = bf16[2,256,3584]{2,1,0:T(8,128)(2,1)} fusion(bf16[1,256,3584]{2,1,0:T(8,128)(2,1)S(1)} %fusion.1, bf16[1,256,3584]{2,1,0:T(8,128)(2,1)S(1)} %fusion), kind=kLoop, calls=%fused_computation.8 | loop fusion | flops 1835008 | bytes 7340032 | tf_op jit(solution)/shard_map/stack | solution.py:219
  10.9 167.0 %shard_map.73 = bf16[2,256,3584]{2,1,0:T(8,128)(2,1)} custom-call(bf16[2,256,3584]{2,1,0:T(8,128)(2,1)} %pad_maximum_fusion.xs_hbm, bf16[3584,512]{1,0:T(8,128)(2,1)} %bitcast.49, bf16[3584,512]{1,0:T(8,128)(2,1)} %bitcast.50, bf16[512,3584]{1,0:T(8,128)(2,1)} %bitcast.51), custom_call_target="tpu_custom_call" | custom-call | tf_op jit(solution)/shard_map/pallas_call | solution.py:158
  177.9 2.6 %fusion.2 = bf16[64,3584]{1,0:T(8,128)(2,1)S(1)} fusion(f32[256,64]{0,1:T(8,128)S(1)} %get-tuple-element.18, bf16[2,256,3584]{2,1,0:T(8,128)(2,1)} %shard_map.73, bf16[1,2,64,3584]{3,2,1,0:T(8,128)(2,1)S(1)} %copy-done), kind=kOutput, calls=%fused_computation.6 | convolution fusion | flops 705331200 | bytes 2818048 | tf_op jit(solution)/shard_map/dot_general | solution.py:222
  180.4 0.2 collective-permute-start
  180.7 2.6 %fusion.3 = bf16[64,3584]{1,0:T(8,128)(2,1)S(1)} fusion(f32[256,64]{0,1:T(8,128)S(1)} %get-tuple-element.10, bf16[2,256,3584]{2,1,0:T(8,128)(2,1)} %shard_map.73, bf16[1,2,64,3584]{3,2,1,0:T(8,128)(2,1)S(1)} %copy-done), kind=kOutput, calls=%fused_computation.7 | convolution fusion | flops 705331200 | bytes 2818048 | tf_op jit(solution)/shard_map/dot_general | solution.py:222
  183.2 2.0 collective-permute-start.1
  185.2 7.3 %collective-permute-done = bf16[64,3584]{1,0:T(8,128)(2,1)S(1)} collective-permute-done((bf16[64,3584]{1,0:T(8,128)(2,1)S(1)}, bf16[64,3584]{1,0:T(8,128)(2,1)S(1)}, u32[]{:S(2)}, u32[]{:S(2)}) %collective-permute-start) | collective-permute-done | bytes 458784 | tf_op jit(solution)/shard_map/ppermute | solution.py:16
  192.5 6.0 %collective-permute-done.1 = bf16[64,3584]{1,0:T(8,128)(2,1)S(1)} collective-permute-done((bf16[64,3584]{1,0:T(8,128)(2,1)S(1)}, bf16[64,3584]{1,0:T(8,128)(2,1)S(1)}, u32[]{:S(2)}, u32[]{:S(2)}) %collective-permute-start.1) | collective-permute-done | bytes 458784 | tf_op jit(solution)/shard_map/ppermute | solution.py:16
  198.5 1.0 maximum_bitcast_fusion
  (2 shorter events, 0.0 us)
Async XLA Ops:
  0.0 8.1 %copy-start = (bf16[1,2,64,3584]{3,2,1,0:T(8,128)(2,1)S(1)}, bf16[1,2,64,3584]{3,2,1,0:T(8,128)(2,1)}, u32[]{:S(2)}) copy-start(bf16[1,2,64,3584]{3,2,1,0:T(8,128)(2,1)} %param.7) | copy-start | bytes 2752516
  180.4 12.0 %collective-permute-start = (bf16[64,3584]{1,0:T(8,128)(2,1)S(1)}, bf16[64,3584]{1,0:T(8,128)(2,1)S(1)}, u32[]{:S(2)}, u32[]{:S(2)}) collective-permute-start(bf16[64,3584]{1,0:T(8,128)(2,1)S(1)} %fusion.2), channel_id=1, source_target_pairs={{0,16},{16,32},{32,48},{48,64},{64,80},{80,96},{96,112},{112,128},... | collective-permute-start | bytes 1376264 | tf_op jit(solution)/shard_map/ppermute | solution.py:16
  183.2 15.2 %collective-permute-start.1 = (bf16[64,3584]{1,0:T(8,128)(2,1)S(1)}, bf16[64,3584]{1,0:T(8,128)(2,1)S(1)}, u32[]{:S(2)}, u32[]{:S(2)}) collective-permute-start(bf16[64,3584]{1,0:T(8,128)(2,1)S(1)} %fusion.3), channel_id=1, source_target_pairs={{0,240},{16,0},{32,16},{48,32},{64,48},{80,64},{96,80},{112,96},{1... | collective-permute-start | bytes 1376264 | tf_op jit(solution)/shard_map/ppermute | solution.py:16

commit v5 on v4

--- a/solution.py
+++ b/solution.py
@@ -20,12 +20,13 @@
 
 
 def moe_kernel(
-    chips, xs_hbm, wg_hbm, wu_hbm, wd_hbm, ys_hbm,
-    recv, res, wg, wu, wd, dsend, drecv, rsend, rrecv, lsem, wsem,
+    chips, xs_hbm, wg_hbm, wu_hbm, wd_hbm, state_ref, hi_ref, lo_ref, next_hbm,
+    recv, res, ys, mixed, wg, wu, wd, dsend, drecv, rsend, rrecv, lsem, wsem, psem,
 ):
     streams, rows, width = recv.shape
     cap = rows // chips
     pipe = lax.axis_index("pipe")
+    pipes = lax.axis_size("pipe")
     me = lax.axis_index("ez")
     core = lax.axis_index("ec")
 
@@ -50,7 +51,10 @@
             barrier, inc=1, device_id=dev(lax.rem(me + k, chips)), device_id_type=MESH
         )
     pl.semaphore_signal(barrier, inc=1, device_id=sibling, device_id_type=MESH)
-    pl.semaphore_wait(barrier, chips)
+    section = (lax.rem(pipe + 1, pipes), lax.rem(pipe + pipes - 1, pipes))
+    for p in section:
+        pl.semaphore_signal(barrier, inc=1, device_id=(p, me, core), device_id_type=MESH)
+    pl.semaphore_wait(barrier, chips + 2)
 
     to_sibling = [
         pltpu.make_async_remote_copy(
@@ -86,7 +90,7 @@
     def back(s, k):
         p = lax.rem(me + k, chips)
         return pltpu.make_async_remote_copy(
-            src_ref=res.at[s, blk(p)], dst_ref=ys_hbm.at[s, blk(me)],
+            src_ref=res.at[s, blk(p)], dst_ref=ys.at[s, blk(me)],
             send_sem=rsend.at[s, k], recv_sem=rrecv.at[s, me],
             device_id=dev(p), device_id_type=MESH,
         )
@@ -94,7 +98,7 @@
     def back_in(s, k):
         q = lax.rem(me + chips - k, chips)
         return pltpu.make_async_remote_copy(
-            src_ref=res.at[s, blk(q)], dst_ref=ys_hbm.at[s, blk(q)],
+            src_ref=res.at[s, blk(q)], dst_ref=ys.at[s, blk(q)],
             send_sem=rsend.at[s, k], recv_sem=rrecv.at[s, q],
             device_id=dev(q), device_id_type=MESH,
         )
@@ -104,7 +108,7 @@
         for s in range(streams)
     ]
     local_out = [
-        pltpu.make_async_copy(res.at[s, blk(me)], ys_hbm.at[s, blk(me)], lsem.at[1, s])
+        pltpu.make_async_copy(res.at[s, blk(me)], ys.at[s, blk(me)], lsem.at[1, s])
         for s in range(streams)
     ]
     for s in range(streams):
@@ -143,26 +147,44 @@
     for s in range(streams):
         for k in range(1, chips):
             dispatch(s, k).wait_send()
+    relay = []
     for s in range(streams):
         local_out[s].wait()
         for k in range(1, chips):
+            back_in(s, k).wait_recv()
+        rows_back = ys[s]
+        total = state_ref[s].astype(jnp.float32)
+        total = total + jnp.dot(hi_ref[s], rows_back, preferred_element_type=jnp.float32)
+        total = total + jnp.dot(lo_ref[s], rows_back, preferred_element_type=jnp.float32)
+        mixed[s] = total.astype(jnp.bfloat16)
+        send = pltpu.make_async_remote_copy(
+            src_ref=mixed.at[s], dst_ref=next_hbm.at[s], send_sem=psem.at[0, s],
+            recv_sem=psem.at[1, s], device_id=(section[s], me, core), device_id_type=MESH,
+        )
+        send.start()
+        relay.append(send)
+    for s in range(streams):
+        for k in range(1, chips):
             back(s, k).wait_send()
-        for k in range(1, chips):
-            back_in(s, k).wait_recv()
-
-
-def expert_pass(outgoing, gate_half, up_half, down_half):
+    for send in relay:
+        send.wait()
+
+
+def expert_pass(outgoing, gate_half, up_half, down_half, state, comb_hi, comb_lo):
     streams, rows, width = outgoing.shape
     chips = lax.axis_size("ez")
     hbm = pl.BlockSpec(memory_space=pl.ANY)
+    vmem = pl.BlockSpec(memory_space=pltpu.VMEM)
     return pl.pallas_call(
         functools.partial(moe_kernel, chips),
-        out_shape=jax.ShapeDtypeStruct(outgoing.shape, jnp.bfloat16),
-        in_specs=[hbm] * 4,
+        out_shape=jax.ShapeDtypeStruct(state.shape, jnp.bfloat16),
+        in_specs=[hbm] * 4 + [vmem] * 3,
         out_specs=hbm,
         scratch_shapes=[
             pltpu.VMEM(outgoing.shape, jnp.bfloat16),
             pltpu.VMEM(outgoing.shape, jnp.bfloat16),
+            pltpu.VMEM(outgoing.shape, jnp.bfloat16),
+            pltpu.VMEM(state.shape, jnp.bfloat16),
             pltpu.VMEM((2,) + gate_half.shape, jnp.bfloat16),
             pltpu.VMEM((2,) + up_half.shape, jnp.bfloat16),
             pltpu.VMEM((2,) + down_half.shape, jnp.bfloat16),
@@ -172,11 +194,12 @@
             pltpu.SemaphoreType.DMA((streams, chips)),
             pltpu.SemaphoreType.DMA((2, streams)),
             pltpu.SemaphoreType.DMA((3, 3)),
+            pltpu.SemaphoreType.DMA((2, streams)),
         ],
         compiler_params=pltpu.CompilerParams(
             collective_id=0, has_side_effects=True, vmem_limit_bytes=62 * 1024 * 1024
         ),
-    )(outgoing, gate_half, up_half, down_half)
+    )(outgoing, gate_half, up_half, down_half, state, comb_hi, comb_lo)
 
 
 def body(streams, norm_gain, w_gate, w_up, w_down, routes, gate_weights):
@@ -189,7 +212,7 @@
     lane_count = experts * capacity
     lane_index = jnp.arange(lane_count, dtype=jnp.int32)
     expert_index = jnp.arange(experts, dtype=jnp.int32)
-    states, outgoings, combines = [], [], []
+    outgoings, combines = [], []
     for stream in range(2):
         state = streams[0, stream].astype(jnp.float32)
         normed = (
@@ -213,22 +236,16 @@
             ),
             axis=-1,
         ).T
-        states.append(state)
         outgoings.append(outgoing)
         combines.append(combine)
-    expert_rows = expert_pass(jnp.stack(outgoings), w_gate[0, 0], w_up[0, 0], w_down[0, 0])
-    results = []
-    for stream in range(2):
-        mixed = states[stream] + jnp.dot(
-            combines[stream],
-            expert_rows[stream].astype(jnp.float32),
-            precision=lax.Precision.HIGHEST,
-            preferred_element_type=jnp.float32,
-        )
-        results.append(mixed.astype(jnp.bfloat16))
-    forward = from_behind(results[0], "pipe", 1)
-    backward = from_behind(results[1], "pipe", -1)
-    return jnp.stack([forward, backward])[None]
+    combine = jnp.stack(combines)
+    comb_hi = combine.astype(jnp.bfloat16)
+    comb_lo = (combine - comb_hi.astype(jnp.float32)).astype(jnp.bfloat16)
+    relayed = expert_pass(
+        jnp.stack(outgoings), w_gate[0, 0], w_up[0, 0], w_down[0, 0],
+        streams[0], comb_hi, comb_lo,
+    )
+    return relayed[None]
 
 
 def solution(mesh):

time: 200 us -> 195 us (0.975)
  waiting for transfers between devices: 13.3 us -> 0 us
  Pallas kernels: 167 us -> 180 us
  matrix products: 7.51 us -> 2.4 us
  starting transfers between devices: 2.18 us -> 0 us
  local copies, waits for them, and re-layouts: 2.3 us -> 4.46 us
    ppermute x2 -> x0, waiting for transfers between devices: 13.3 us -> none  [from_behind(): return lax.ppermute(value, axis, pairs)]
    pallas_call x1, Pallas kernels: 167 us -> 180 us  [expert_pass(): pl.pallas_call(functools.partial(moe_kernel, chips), out_shape=jax.ShapeD...]
    dot_general x2 -> x0, matrix products: 5.11 us -> none  [body(): jnp.dot(combines[stream], expert_rows[stream].astype(jnp.float32), precis...]
    ppermute x2 -> x0, starting transfers between devices: 2.18 us -> none  [from_behind(): return lax.ppermute(value, axis, pairs)]
    unnamed x2 -> x3, local copies, waits for them, and re-layouts: 0.01 us -> 2.16 us
  transfers between devices with their start and end apart: 2 -> 0, of which waited for: 2 -> 0; matrix products, arithmetic and copies ran while one was open for 1% -> 0% of each run, Pallas kernels for 0% -> 0%
where the time goes in v5:
time: 195 us; the launch traced here: 194 us
  Pallas kernels  180 us (92%)
  other arithmetic  7.38 us (4%)
  local copies, waits for them, and re-layouts  4.46 us (2%)
  matrix products  2.4 us (1%)
    pallas_call x1, Pallas kernels, expert_pass(): pl.pallas_call(functools.partial(moe_kernel, chips), out_shape=jax.ShapeD...  180 us

profile of v5, /device:TPU:30, one launch (start us, length us, event | category | flops | bytes accessed | tf_op | source)
XLA Modules:
  0.0 194.1 jit_solution(6649870600137135531)
XLA Ops:
  0.0 0.0 copy-start
  0.0 1.5 fusion.2
  1.5 0.7 slice_bitcast_fusion.1
  2.2 0.7 fusion.23
  2.9 0.8 reduce
  3.7 0.1 copy.24
  3.8 0.1 eq.61
  3.9 0.1 copy.26
  4.0 0.1 eq.68
  4.2 0.1 fusion.19
  4.3 0.2 reduce_window_sum.18
  4.4 0.2 select_reduce_fusion.2
  4.6 0.1 reduce_sum.81
  4.8 0.1 copy.27
  4.8 0.1 fusion.20
  4.9 0.2 reduce_window_sum.17
  5.1 0.2 select_reduce_fusion.3
  5.3 0.1 reduce_sum.77
  5.4 0.1 copy.25
  5.5 0.7 bitcast_add_fusion.1
  6.2 0.1 select_reduce_fusion
  6.4 0.6 subtract_convert_fusion.lo_ref
  7.0 0.6 fusion.18.hi_ref
  7.6 1.7 fusion.1
  9.3 0.0 copy-done
  9.4 0.7 fusion
  10.1 2.1 %pad_maximum_fusion.xs_hbm = bf16[2,256,3584]{2,1,0:T(8,128)(2,1)} fusion(bf16[1,256,3584]{2,1,0:T(8,128)(2,1)S(1)} %fusion.1, bf16[1,256,3584]{2,1,0:T(8,128)(2,1)S(1)} %fusion), kind=kLoop, calls=%fused_computation.4 | loop fusion | flops 1835008 | bytes 7340032 | tf_op jit(solution)/shard_map/stack | solution.py:245
  12.2 179.8 %shard_map.73 = bf16[2,64,3584]{2,1,0:T(8,128)(2,1)} custom-call(bf16[2,256,3584]{2,1,0:T(8,128)(2,1)} %pad_maximum_fusion.xs_hbm, bf16[3584,512]{1,0:T(8,128)(2,1)} %bitcast.45, bf16[3584,512]{1,0:T(8,128)(2,1)} %bitcast.46, bf16[512,3584]{1,0:T(8,128)(2,1)} %bitcast.47, bf16[2,64,3584]{2,1,0:T(8,128)(2,1)} %bitcast.43, bf16[2,64,256]{2,1,0:T(8,128)(2,1)} %fusion.18.hi_ref, ...), custom_call_target="tpu_custom_call" | custom-call | tf_op jit(solution)/shard_map/pallas_call | solution.py:178
  192.0 2.2 %copy.29 = bf16[1,2,64,3584]{3,2,1,0:T(8,128)(2,1)} copy(bf16[1,2,64,3584]{3,2,1,0:T(8,128)(2,1)} %bitcast.44) | data formatting | bytes 1835008
  (1 shorter events, 0.0 us)
Async XLA Ops:
  0.0 9.3 %copy-start = (bf16[1,2,64,3584]{3,2,1,0:T(8,128)(2,1)S(1)}, bf16[1,2,64,3584]{3,2,1,0:T(8,128)(2,1)}, u32[]{:S(2)}) copy-start(bf16[1,2,64,3584]{3,2,1,0:T(8,128)(2,1)} %param.7) | copy-start | bytes 2752516

commit v6 on v5

--- a/solution.py
+++ b/solution.py
@@ -111,10 +111,17 @@
         pltpu.make_async_copy(res.at[s, blk(me)], ys.at[s, blk(me)], lsem.at[1, s])
         for s in range(streams)
     ]
-    for s in range(streams):
+    def send_rows(s):
         local_in[s].start()
         for k in range(1, chips):
             dispatch(s, k).start()
+
+    def rows_arrived(s):
+        local_in[s].wait()
+        for k in range(1, chips):
+            dispatch_in(s, k).wait_recv()
+
+    send_rows(0)
     for c in to_sibling:
         c.start()
     for c in own_copies:
@@ -125,10 +132,12 @@
         c.wait_send()
 
     tile = 128
-    for s in range(streams):
-        local_in[s].wait()
-        for k in range(1, chips):
-            dispatch_in(s, k).wait_recv()
+    rows_arrived(0)
+    for s in range(streams):
+        if s + 1 < streams:
+            send_rows(s + 1)
+        if s > 0:
+            rows_arrived(s)
         for b in range(rows // tile):
             x = recv[s, pl.ds(b * tile, tile), :]
             total = None

time: 195 us -> 198 us (1.015); the launches traced: 194 us -> 195 us
  no operation moved by 1% of the time
where the time goes in v6:
time: 198 us; the launch traced here: 195 us
  Pallas kernels  181 us (91%)
  other arithmetic  7.38 us (4%)
  local copies, waits for them, and re-layouts  4.46 us (2%)
  matrix products  2.4 us (1%)
    pallas_call x1, Pallas kernels, expert_pass(): pl.pallas_call(functools.partial(moe_kernel, chips), out_shape=jax.ShapeD...  181 us

profile of v6, /device:TPU:30, one launch (start us, length us, event | category | flops | bytes accessed | tf_op | source)
XLA Modules:
  0.0 194.9 jit_solution(9005121880318684491)
XLA Ops:
  0.0 0.0 copy-start
  0.0 1.5 fusion.2
  1.5 0.7 slice_bitcast_fusion.1
  2.2 0.7 fusion.23
  2.9 0.8 reduce
  3.7 0.1 copy.24
  3.8 0.1 eq.61
  3.9 0.1 copy.26
  4.0 0.1 eq.68
  4.2 0.1 fusion.19
  4.3 0.2 reduce_window_sum.18
  4.4 0.2 select_reduce_fusion.2
  4.6 0.1 reduce_sum.81
  4.8 0.1 copy.27
  4.8 0.1 fusion.20
  4.9 0.2 reduce_window_sum.17
  5.1 0.2 select_reduce_fusion.3
  5.3 0.1 reduce_sum.77
  5.4 0.1 copy.25
  5.5 0.7 bitcast_add_fusion.1
  6.2 0.1 select_reduce_fusion
  6.4 0.6 subtract_convert_fusion.lo_ref
  7.0 0.6 fusion.18.hi_ref
  7.6 1.7 fusion.1
  9.3 0.0 copy-done
  9.4 0.7 fusion
  10.1 2.1 %pad_maximum_fusion.xs_hbm = bf16[2,256,3584]{2,1,0:T(8,128)(2,1)} fusion(bf16[1,256,3584]{2,1,0:T(8,128)(2,1)S(1)} %fusion.1, bf16[1,256,3584]{2,1,0:T(8,128)(2,1)S(1)} %fusion), kind=kLoop, calls=%fused_computation.4 | loop fusion | flops 1835008 | bytes 7340032 | tf_op jit(solution)/shard_map/stack | solution.py:254
  12.2 180.6 %shard_map.73 = bf16[2,64,3584]{2,1,0:T(8,128)(2,1)} custom-call(bf16[2,256,3584]{2,1,0:T(8,128)(2,1)} %pad_maximum_fusion.xs_hbm, bf16[3584,512]{1,0:T(8,128)(2,1)} %bitcast.45, bf16[3584,512]{1,0:T(8,128)(2,1)} %bitcast.46, bf16[512,3584]{1,0:T(8,128)(2,1)} %bitcast.47, bf16[2,64,3584]{2,1,0:T(8,128)(2,1)} %bitcast.43, bf16[2,64,256]{2,1,0:T(8,128)(2,1)} %fusion.18.hi_ref, ...), custom_call_target="tpu_custom_call" | custom-call | tf_op jit(solution)/shard_map/pallas_call | solution.py:187
  192.8 2.2 %copy.29 = bf16[1,2,64,3584]{3,2,1,0:T(8,128)(2,1)} copy(bf16[1,2,64,3584]{3,2,1,0:T(8,128)(2,1)} %bitcast.44) | data formatting | bytes 1835008
  (1 shorter events, 0.0 us)
Async XLA Ops:
  0.0 9.3 %copy-start = (bf16[1,2,64,3584]{3,2,1,0:T(8,128)(2,1)S(1)}, bf16[1,2,64,3584]{3,2,1,0:T(8,128)(2,1)}, u32[]{:S(2)}) copy-start(bf16[1,2,64,3584]{3,2,1,0:T(8,128)(2,1)} %param.7) | copy-start | bytes 2752516

commit v7 on v6

--- a/solution.py
+++ b/solution.py
@@ -21,7 +21,7 @@
 
 def moe_kernel(
     chips, xs_hbm, wg_hbm, wu_hbm, wd_hbm, state_ref, hi_ref, lo_ref, next_hbm,
-    recv, res, ys, mixed, wg, wu, wd, dsend, drecv, rsend, rrecv, lsem, wsem, psem,
+    recv, res, ys, mixed, rbuf, wg, wu, wd, dsend, drecv, rsend, rrecv, lsem, wsem, psem, rsem,
 ):
     streams, rows, width = recv.shape
     cap = rows // chips
@@ -103,6 +103,61 @@
             device_id=dev(q), device_id_type=MESH,
         )
 
+    anti = chips // 2
+    half = cap // 2
+    send_from = (xs_hbm, res)
+    land_in = (recv, ys)
+
+    def half_rows(q, h):
+        return pl.ds(pl.multiple_of(q * cap + h * half, half), half)
+
+    def via(h):
+        return lax.rem(me + (anti - 1 if h == 0 else chips - anti + 1), chips)
+
+    def relay_out(ph, s, h):
+        return pltpu.make_async_remote_copy(
+            src_ref=send_from[ph].at[s, half_rows(lax.rem(me + anti, chips), h)],
+            dst_ref=rbuf.at[ph, s, h], send_sem=rsem.at[0, ph, s, h],
+            recv_sem=rsem.at[1, ph, s, h], device_id=dev(via(h)), device_id_type=MESH,
+        )
+
+    def forward(ph, s, h):
+        step = 1 if h == 0 else chips - 1
+        origin = lax.rem(me + chips - anti + 1, chips) if h == 0 else lax.rem(me + anti - 1, chips)
+        return pltpu.make_async_remote_copy(
+            src_ref=rbuf.at[ph, s, h], dst_ref=land_in[ph].at[s, half_rows(origin, h)],
+            send_sem=rsem.at[2, ph, s, h], recv_sem=rsem.at[3, ph, s, h],
+            device_id=dev(lax.rem(me + step, chips)), device_id_type=MESH,
+        )
+
+    def forward_in(ph, s, h):
+        origin = lax.rem(me + anti, chips)
+        return pltpu.make_async_remote_copy(
+            src_ref=rbuf.at[ph, s, h], dst_ref=land_in[ph].at[s, half_rows(origin, h)],
+            send_sem=rsem.at[2, ph, s, h], recv_sem=rsem.at[3, ph, s, h],
+            device_id=dev(origin), device_id_type=MESH,
+        )
+
+    def relay_start(ph, s):
+        for h in range(2):
+            relay_out(ph, s, h).start()
+
+    def relay_pass_on(ph, s):
+        for h in range(2):
+            relay_out(ph, s, h).wait_recv()
+            forward(ph, s, h).start()
+
+    def relay_landed(ph, s):
+        for h in range(2):
+            forward_in(ph, s, h).wait_recv()
+
+    def relay_done(ph, s):
+        for h in range(2):
+            relay_out(ph, s, h).wait_send()
+            forward(ph, s, h).wait_send()
+
+    direct = [k for k in range(1, chips) if k != anti]
+
     local_in = [
         pltpu.make_async_copy(xs_hbm.at[s, blk(me)], recv.at[s, blk(me)], lsem.at[0, s])
         for s in range(streams)
@@ -113,15 +168,19 @@
     ]
     def send_rows(s):
         local_in[s].start()
-        for k in range(1, chips):
+        relay_start(0, s)
+        for k in direct:
             dispatch(s, k).start()
 
     def rows_arrived(s):
+        relay_pass_on(0, s)
         local_in[s].wait()
-        for k in range(1, chips):
+        for k in direct:
             dispatch_in(s, k).wait_recv()
-
-    send_rows(0)
+        relay_landed(0, s)
+
+    for s in range(streams):
+        send_rows(s)
     for c in to_sibling:
         c.start()
     for c in own_copies:
@@ -132,12 +191,8 @@
         c.wait_send()
 
     tile = 128
-    rows_arrived(0)
-    for s in range(streams):
-        if s + 1 < streams:
-            send_rows(s + 1)
-        if s > 0:
-            rows_arrived(s)
+    for s in range(streams):
+        rows_arrived(s)
         for b in range(rows // tile):
             x = recv[s, pl.ds(b * tile, tile), :]
             total = None
@@ -150,17 +205,20 @@
                 total = part if total is None else total + part
             res[s, pl.ds(b * tile, tile), :] = total.astype(jnp.bfloat16)
         local_out[s].start()
-        for k in range(1, chips):
+        relay_start(1, s)
+        for k in direct:
             back(s, k).start()
 
     for s in range(streams):
-        for k in range(1, chips):
+        for k in direct:
             dispatch(s, k).wait_send()
     relay = []
     for s in range(streams):
+        relay_pass_on(1, s)
         local_out[s].wait()
-        for k in range(1, chips):
+        for k in direct:
             back_in(s, k).wait_recv()
+        relay_landed(1, s)
         rows_back = ys[s]
         total = state_ref[s].astype(jnp.float32)
         total = total + jnp.dot(hi_ref[s], rows_back, preferred_element_type=jnp.float32)
@@ -173,8 +231,10 @@
         send.start()
         relay.append(send)
     for s in range(streams):
-        for k in range(1, chips):
+        for k in direct:
             back(s, k).wait_send()
+        for ph in range(2):
+            relay_done(ph, s)
     for send in relay:
         send.wait()
 
@@ -194,6 +254,7 @@
             pltpu.VMEM(outgoing.shape, jnp.bfloat16),
             pltpu.VMEM(outgoing.shape, jnp.bfloat16),
             pltpu.VMEM(state.shape, jnp.bfloat16),
+            pltpu.VMEM((2, streams, 2, rows // chips // 2, width), jnp.bfloat16),
             pltpu.VMEM((2,) + gate_half.shape, jnp.bfloat16),
             pltpu.VMEM((2,) + up_half.shape, jnp.bfloat16),
             pltpu.VMEM((2,) + down_half.shape, jnp.bfloat16),
@@ -204,6 +265,7 @@
             pltpu.SemaphoreType.DMA((2, streams)),
             pltpu.SemaphoreType.DMA((3, 3)),
             pltpu.SemaphoreType.DMA((2, streams)),
+            pltpu.SemaphoreType.DMA((4, 2, streams, 2)),
         ],
         compiler_params=pltpu.CompilerParams(
             collective_id=0, has_side_effects=True, vmem_limit_bytes=62 * 1024 * 1024

time: 198 us -> 216 us (1.091); the launches traced: 195 us -> 216 us
  Pallas kernels: 181 us -> 202 us
    pallas_call x1, Pallas kernels: 181 us -> 202 us  [expert_pass(): pl.pallas_call(functools.partial(moe_kernel, chips), out_shape=jax.ShapeD...]
where the time goes in v7:
time: 216 us
  Pallas kernels  202 us (94%)
  other arithmetic  7.38 us (3%)
  local copies, waits for them, and re-layouts  4.46 us (2%)
  matrix products  2.4 us (1%)
    pallas_call x1, Pallas kernels, expert_pass(): pl.pallas_call(functools.partial(moe_kernel, chips), out_shape=jax.ShapeD...  202 us

profile of v7, /device:TPU:30, one launch (start us, length us, event | category | flops | bytes accessed | tf_op | source)
XLA Modules:
  0.0 216.0 jit_solution(11776664148253191928)
XLA Ops:
  0.0 0.0 copy-start
  0.0 1.5 fusion.2
  1.5 0.7 slice_bitcast_fusion.1
  2.2 0.7 fusion.23
  2.9 0.8 reduce
  3.7 0.1 copy.24
  3.8 0.1 eq.61
  3.9 0.1 copy.26
  4.0 0.1 eq.68
  4.2 0.1 fusion.19
  4.3 0.2 reduce_window_sum.18
  4.4 0.2 select_reduce_fusion.2
  4.6 0.1 reduce_sum.81
  4.8 0.1 copy.27
  4.8 0.1 fusion.20
  4.9 0.2 reduce_window_sum.17
  5.1 0.2 select_reduce_fusion.3
  5.3 0.1 reduce_sum.77
  5.4 0.1 copy.25
  5.5 0.7 bitcast_add_fusion.1
  6.2 0.1 select_reduce_fusion
  6.4 0.6 subtract_convert_fusion.lo_ref
  7.0 0.6 fusion.18.hi_ref
  7.6 1.7 fusion.1
  9.3 0.0 copy-done
  9.4 0.7 fusion
  10.1 2.1 pad_maximum_fusion.xs_hbm
  12.2 201.6 %shard_map.73 = bf16[2,64,3584]{2,1,0:T(8,128)(2,1)} custom-call(bf16[2,256,3584]{2,1,0:T(8,128)(2,1)} %pad_maximum_fusion.xs_hbm, bf16[3584,512]{1,0:T(8,128)(2,1)} %bitcast.45, bf16[3584,512]{1,0:T(8,128)(2,1)} %bitcast.46, bf16[512,3584]{1,0:T(8,128)(2,1)} %bitcast.47, bf16[2,64,3584]{2,1,0:T(8,128)(2,1)} %bitcast.43, bf16[2,64,256]{2,1,0:T(8,128)(2,1)} %fusion.18.hi_ref, ...), custom_call_target="tpu_custom_call" | custom-call | tf_op jit(solution)/shard_map/pallas_call | solution.py:247
  213.8 2.2 %copy.29 = bf16[1,2,64,3584]{3,2,1,0:T(8,128)(2,1)} copy(bf16[1,2,64,3584]{3,2,1,0:T(8,128)(2,1)} %bitcast.44) | data formatting | bytes 1835008
  (1 shorter events, 0.0 us)
Async XLA Ops:
  0.0 9.3 %copy-start = (bf16[1,2,64,3584]{3,2,1,0:T(8,128)(2,1)S(1)}, bf16[1,2,64,3584]{3,2,1,0:T(8,128)(2,1)}, u32[]{:S(2)}) copy-start(bf16[1,2,64,3584]{3,2,1,0:T(8,128)(2,1)} %param.7) | copy-start | bytes 2752516

commit v8 on v5

--- a/solution.py
+++ b/solution.py
@@ -20,8 +20,8 @@
 
 
 def moe_kernel(
-    chips, xs_hbm, wg_hbm, wu_hbm, wd_hbm, state_ref, hi_ref, lo_ref, next_hbm,
-    recv, res, ys, mixed, wg, wu, wd, dsend, drecv, rsend, rrecv, lsem, wsem, psem,
+    chips, wg_hbm, wu_hbm, wd_hbm, state_ref, gain_ref, pick_ref, hi_ref, lo_ref, next_hbm,
+    xs, recv, res, ys, mixed, wg, wu, wd, dsend, drecv, rsend, rrecv, lsem, wsem, psem,
 ):
     streams, rows, width = recv.shape
     cap = rows // chips
@@ -74,7 +74,7 @@
     def dispatch(s, k):
         p = lax.rem(me + k, chips)
         return pltpu.make_async_remote_copy(
-            src_ref=xs_hbm.at[s, blk(p)], dst_ref=recv.at[s, blk(me)],
+            src_ref=xs.at[s, blk(p)], dst_ref=recv.at[s, blk(me)],
             send_sem=dsend.at[s, k], recv_sem=drecv.at[s, me],
             device_id=dev(p), device_id_type=MESH,
         )
@@ -82,7 +82,7 @@
     def dispatch_in(s, k):
         q = lax.rem(me + chips - k, chips)
         return pltpu.make_async_remote_copy(
-            src_ref=xs_hbm.at[s, blk(q)], dst_ref=recv.at[s, blk(q)],
+            src_ref=xs.at[s, blk(q)], dst_ref=recv.at[s, blk(q)],
             send_sem=dsend.at[s, k], recv_sem=drecv.at[s, q],
             device_id=dev(q), device_id_type=MESH,
         )
@@ -104,7 +104,7 @@
         )
 
     local_in = [
-        pltpu.make_async_copy(xs_hbm.at[s, blk(me)], recv.at[s, blk(me)], lsem.at[0, s])
+        pltpu.make_async_copy(xs.at[s, blk(me)], recv.at[s, blk(me)], lsem.at[0, s])
         for s in range(streams)
     ]
     local_out = [
@@ -112,6 +112,12 @@
         for s in range(streams)
     ]
     for s in range(streams):
+        state = state_ref[s].astype(jnp.float32)
+        scale = lax.rsqrt(jnp.mean(state * state, axis=-1, keepdims=True) + 1e-06)
+        normed = (state * scale * gain_ref[...]).astype(jnp.bfloat16)
+        xs[s] = jnp.dot(pick_ref[s], normed, preferred_element_type=jnp.float32).astype(
+            jnp.bfloat16
+        )
         local_in[s].start()
         for k in range(1, chips):
             dispatch(s, k).start()
@@ -170,20 +176,23 @@
         send.wait()
 
 
-def expert_pass(outgoing, gate_half, up_half, down_half, state, comb_hi, comb_lo):
-    streams, rows, width = outgoing.shape
+def expert_pass(pick, gate_half, up_half, down_half, state, gain, comb_hi, comb_lo):
+    streams, rows, _ = pick.shape
+    width = state.shape[-1]
     chips = lax.axis_size("ez")
     hbm = pl.BlockSpec(memory_space=pl.ANY)
     vmem = pl.BlockSpec(memory_space=pltpu.VMEM)
+    lanes = (streams, rows, width)
     return pl.pallas_call(
         functools.partial(moe_kernel, chips),
         out_shape=jax.ShapeDtypeStruct(state.shape, jnp.bfloat16),
-        in_specs=[hbm] * 4 + [vmem] * 3,
+        in_specs=[hbm] * 3 + [vmem] * 5,
         out_specs=hbm,
         scratch_shapes=[
-            pltpu.VMEM(outgoing.shape, jnp.bfloat16),
-            pltpu.VMEM(outgoing.shape, jnp.bfloat16),
-            pltpu.VMEM(outgoing.shape, jnp.bfloat16),
+            pltpu.VMEM(lanes, jnp.bfloat16),
+            pltpu.VMEM(lanes, jnp.bfloat16),
+            pltpu.VMEM(lanes, jnp.bfloat16),
+            pltpu.VMEM(lanes, jnp.bfloat16),
             pltpu.VMEM(state.shape, jnp.bfloat16),
             pltpu.VMEM((2,) + gate_half.shape, jnp.bfloat16),
             pltpu.VMEM((2,) + up_half.shape, jnp.bfloat16),
@@ -199,12 +208,11 @@
         compiler_params=pltpu.CompilerParams(
             collective_id=0, has_side_effects=True, vmem_limit_bytes=62 * 1024 * 1024
         ),
-    )(outgoing, gate_half, up_half, down_half, state, comb_hi, comb_lo)
+    )(gate_half, up_half, down_half, state, gain, pick, comb_hi, comb_lo)
 
 
 def body(streams, norm_gain, w_gate, w_up, w_down, routes, gate_weights):
     experts = lax.axis_size("ez")
-    gain_row = norm_gain[0]
     tok_rows = streams.shape[2]
     width = streams.shape[3]
     top_count = routes.shape[3]
@@ -214,10 +222,6 @@
     expert_index = jnp.arange(experts, dtype=jnp.int32)
     outgoings, combines = [], []
     for stream in range(2):
-        state = streams[0, stream].astype(jnp.float32)
-        normed = (
-            state * lax.rsqrt(jnp.mean(state * state, axis=-1, keepdims=True) + 1e-06) * gain_row
-        ).astype(jnp.bfloat16)
         chosen = routes[0, stream].reshape(-1)
         onehot = (chosen[:, None] == expert_index[None, :]).astype(jnp.int32)
         slot_rank = jnp.sum((jnp.cumsum(onehot, axis=0) - onehot) * onehot, axis=1)
@@ -226,9 +230,6 @@
         send_matrix = jnp.sum(
             matches.reshape(lane_count, tok_rows, top_count).astype(jnp.float32), axis=-1
         ).astype(jnp.bfloat16)
-        outgoing = jnp.dot(send_matrix, normed, preferred_element_type=jnp.float32).astype(
-            jnp.bfloat16
-        )
         weights = gate_weights[0, stream].reshape(-1)
         combine = jnp.sum(
             (matches.astype(jnp.float32) * weights[None, :]).reshape(
@@ -236,14 +237,14 @@
             ),
             axis=-1,
         ).T
-        outgoings.append(outgoing)
+        outgoings.append(send_matrix)
         combines.append(combine)
     combine = jnp.stack(combines)
     comb_hi = combine.astype(jnp.bfloat16)
     comb_lo = (combine - comb_hi.astype(jnp.float32)).astype(jnp.bfloat16)
     relayed = expert_pass(
         jnp.stack(outgoings), w_gate[0, 0], w_up[0, 0], w_down[0, 0],
-        streams[0], comb_hi, comb_lo,
+        streams[0], norm_gain, comb_hi, comb_lo,
     )
     return relayed[None]
 

time: 195 us -> 190 us (0.974)
  other arithmetic: 7.38 us -> 3.69 us
  matrix products: 2.4 us -> 0 us
    dot_general x2 -> x0, matrix products: 2.4 us -> none  [body(): jnp.dot(send_matrix, normed, preferred_element_type=jnp.float32)]
where the time goes in v8:
time: 190 us; the launch traced here: 189 us
  Pallas kernels  181 us (95%)
  local copies, waits for them, and re-layouts  4.68 us (2%)
  other arithmetic  3.69 us (2%)
    pallas_call x1, Pallas kernels, expert_pass(): pl.pallas_call(functools.partial(moe_kernel, chips), out_shape=jax.ShapeD...  181 us

profile of v8, /device:TPU:30, one launch (start us, length us, event | category | flops | bytes accessed | tf_op | source)
XLA Modules:
  0.0 189.1 jit_solution(12790389558158113836)
XLA Ops:
  0.0 0.7 slice_bitcast_fusion.1
  0.7 0.7 fusion.3
  1.4 0.1 copy.24
  1.5 0.1 eq.61
  1.6 0.1 copy.27
  1.7 0.1 eq.68
  1.9 0.1 fusion.1
  2.0 0.2 reduce_window_sum.18
  2.1 0.2 select_reduce_fusion.2
  2.3 0.1 reduce_sum.62
  2.5 0.1 copy.28
  2.5 0.1 fusion.2
  2.6 0.2 reduce_window_sum.17
  2.8 0.2 select_reduce_fusion.3
  3.0 0.1 reduce_sum.59
  3.1 0.1 copy.25
  3.2 0.7 bitcast_add_fusion.1
  3.9 0.1 select_reduce_fusion
  4.1 0.6 subtract_convert_fusion.lo_ref
  4.7 0.6 fusion.hi_ref
  5.3 0.1 copy.29
  5.5 0.1 copy.26
  5.6 0.7 pad_maximum_fusion.pick_ref
  6.3 180.7 %shard_map.73 = bf16[2,64,3584]{2,1,0:T(8,128)(2,1)} custom-call(bf16[3584,512]{1,0:T(8,128)(2,1)} %bitcast.30, bf16[3584,512]{1,0:T(8,128)(2,1)} %bitcast.31, bf16[512,3584]{1,0:T(8,128)(2,1)} %bitcast.32, bf16[2,64,3584]{2,1,0:T(8,128)(2,1)} %bitcast.33, f32[1,3584]{1,0:T(1,128)} %gain_ref.1, bf16[2,256,64]{2,1,0:T(8,128)(2,1)} %pad_maximum_fusion.pick_ref, ...), custom_call_target="tpu_custom_call" | custom-call | tf_op jit(solution)/shard_map/pallas_call | solution.py:186
  187.0 2.2 %copy.31 = bf16[1,2,64,3584]{3,2,1,0:T(8,128)(2,1)} copy(bf16[1,2,64,3584]{3,2,1,0:T(8,128)(2,1)} %bitcast.29) | data formatting | bytes 1835008

commit v9 on v8

--- a/solution.py
+++ b/solution.py
@@ -213,37 +213,22 @@
 
 def body(streams, norm_gain, w_gate, w_up, w_down, routes, gate_weights):
     experts = lax.axis_size("ez")
-    tok_rows = streams.shape[2]
-    width = streams.shape[3]
-    top_count = routes.shape[3]
+    _, stream_count, tok_rows, top_count = routes.shape
     capacity = 2 * tok_rows * top_count // experts
     lane_count = experts * capacity
-    lane_index = jnp.arange(lane_count, dtype=jnp.int32)
-    expert_index = jnp.arange(experts, dtype=jnp.int32)
-    outgoings, combines = [], []
-    for stream in range(2):
-        chosen = routes[0, stream].reshape(-1)
-        onehot = (chosen[:, None] == expert_index[None, :]).astype(jnp.int32)
-        slot_rank = jnp.sum((jnp.cumsum(onehot, axis=0) - onehot) * onehot, axis=1)
-        lane_of = chosen * capacity + slot_rank
-        matches = lane_index[:, None] == lane_of[None, :]
-        send_matrix = jnp.sum(
-            matches.reshape(lane_count, tok_rows, top_count).astype(jnp.float32), axis=-1
-        ).astype(jnp.bfloat16)
-        weights = gate_weights[0, stream].reshape(-1)
-        combine = jnp.sum(
-            (matches.astype(jnp.float32) * weights[None, :]).reshape(
-                lane_count, tok_rows, top_count
-            ),
-            axis=-1,
-        ).T
-        outgoings.append(send_matrix)
-        combines.append(combine)
-    combine = jnp.stack(combines)
+    pairs = tok_rows * top_count
+    chosen = routes[0].reshape(stream_count, pairs)
+    earlier = jnp.arange(pairs)[None, :] < jnp.arange(pairs)[:, None]
+    same = (chosen[:, :, None] == chosen[:, None, :]) & earlier[None]
+    slot_rank = jnp.sum(same.astype(jnp.int32), axis=-1)
+    lane_of = (chosen * capacity + slot_rank).reshape(stream_count, tok_rows, top_count)
+    matches = lane_of[..., None] == jnp.arange(lane_count, dtype=jnp.int32)
+    pick = jnp.any(matches, axis=2).astype(jnp.bfloat16).transpose(0, 2, 1)
+    combine = jnp.sum(jnp.where(matches, gate_weights[0][..., None], 0.0), axis=2)
     comb_hi = combine.astype(jnp.bfloat16)
     comb_lo = (combine - comb_hi.astype(jnp.float32)).astype(jnp.bfloat16)
     relayed = expert_pass(
-        jnp.stack(outgoings), w_gate[0, 0], w_up[0, 0], w_down[0, 0],
+        pick, w_gate[0, 0], w_up[0, 0], w_down[0, 0],
         streams[0], norm_gain, comb_hi, comb_lo,
     )
     return relayed[None]

time: 190 us -> 188 us (0.989)
  no operation moved by 1% of the time
where the time goes in v9:
time: 188 us; the launch traced here: 187 us
  Pallas kernels  181 us (96%)
  local copies, waits for them, and re-layouts  4.07 us (2%)
    pallas_call x1, Pallas kernels, expert_pass(): pl.pallas_call(functools.partial(moe_kernel, chips), out_shape=jax.ShapeD...  181 us

profile of v9, /device:TPU:30, one launch (start us, length us, event | category | flops | bytes accessed | tf_op | source)
XLA Modules:
  0.0 186.7 jit_solution(7713932476845362788)
XLA Ops:
  0.0 0.8 copy.17
  0.8 0.1 eq.28
  0.9 0.2 convert_reduce_fusion
  1.1 0.1 reduce_sum.21
  1.3 0.1 copy.19
  1.4 0.1 fusion
  1.5 0.8 copy.20
  2.3 0.8 select_reduce_fusion
  3.1 0.7 subtract_convert_fusion
  3.8 180.7 %shard_map.73 = bf16[2,64,3584]{2,1,0:T(8,128)(2,1)} custom-call(bf16[3584,512]{1,0:T(8,128)(2,1)} %bitcast.12, bf16[3584,512]{1,0:T(8,128)(2,1)} %bitcast.13, bf16[512,3584]{1,0:T(8,128)(2,1)} %bitcast.14, bf16[2,64,3584]{2,1,0:T(8,128)(2,1)} %bitcast.15, f32[1,3584]{1,0:T(1,128)} %gain_ref.1, bf16[2,256,64]{2,1,0:T(8,128)(2,1)} %bitcast.16, ...), custom_call_target="tpu_custom_call" | custom-call | tf_op jit(solution)/shard_map/pallas_call | solution.py:186
  184.5 2.2 %copy.22 = bf16[1,2,64,3584]{3,2,1,0:T(8,128)(2,1)} copy(bf16[1,2,64,3584]{3,2,1,0:T(8,128)(2,1)} %bitcast.11) | data formatting | bytes 1835008
  (3 shorter events, 0.0 us)

commit v10 on v9

--- a/solution.py
+++ b/solution.py
@@ -42,9 +42,6 @@
         pltpu.make_async_copy(src, dst.at[core], wsem.at[0, i])
         for i, (src, dst) in enumerate(weights)
     ]
-    for c in own_copies:
-        c.start()
-
     barrier = pltpu.get_barrier_semaphore()
     for k in range(1, chips):
         pl.semaphore_signal(
@@ -121,6 +118,8 @@
         local_in[s].start()
         for k in range(1, chips):
             dispatch(s, k).start()
+    for c in own_copies:
+        c.start()
     for c in to_sibling:
         c.start()
     for c in own_copies:

time: 188 us -> 188 us (level)
  no operation moved by 1% of the time
where the time goes in v10:
time: 188 us; the launch traced here: 187 us
  Pallas kernels  181 us (96%)
  local copies, waits for them, and re-layouts  4.07 us (2%)
    pallas_call x1, Pallas kernels, expert_pass(): pl.pallas_call(functools.partial(moe_kernel, chips), out_shape=jax.ShapeD...  181 us

profile of v10, /device:TPU:30, one launch (start us, length us, event | category | flops | bytes accessed | tf_op | source)
XLA Modules:
  0.0 186.7 jit_solution(8296454081812669297)
XLA Ops:
  0.0 0.8 copy.17
  0.8 0.1 eq.28
  0.9 0.2 convert_reduce_fusion
  1.1 0.1 reduce_sum.21
  1.3 0.1 copy.19
  1.4 0.1 fusion
  1.5 0.8 copy.20
  2.3 0.8 select_reduce_fusion
  3.1 0.7 subtract_convert_fusion
  3.8 180.7 %shard_map.73 = bf16[2,64,3584]{2,1,0:T(8,128)(2,1)} custom-call(bf16[3584,512]{1,0:T(8,128)(2,1)} %bitcast.12, bf16[3584,512]{1,0:T(8,128)(2,1)} %bitcast.13, bf16[512,3584]{1,0:T(8,128)(2,1)} %bitcast.14, bf16[2,64,3584]{2,1,0:T(8,128)(2,1)} %bitcast.15, f32[1,3584]{1,0:T(1,128)} %gain_ref.1, bf16[2,256,64]{2,1,0:T(8,128)(2,1)} %bitcast.16, ...), custom_call_target="tpu_custom_call" | custom-call | tf_op jit(solution)/shard_map/pallas_call | solution.py:185
  184.5 2.2 %copy.22 = bf16[1,2,64,3584]{3,2,1,0:T(8,128)(2,1)} copy(bf16[1,2,64,3584]{3,2,1,0:T(8,128)(2,1)} %bitcast.11) | data formatting | bytes 1835008
  (3 shorter events, 0.0 us)

commit v11 on v9

--- a/solution.py
+++ b/solution.py
@@ -45,6 +45,15 @@
     for c in own_copies:
         c.start()
 
+    def select_rows(s):
+        state = state_ref[s].astype(jnp.float32)
+        scale = lax.rsqrt(jnp.mean(state * state, axis=-1, keepdims=True) + 1e-06)
+        normed = (state * scale * gain_ref[...]).astype(jnp.bfloat16)
+        xs[s] = jnp.dot(pick_ref[s], normed, preferred_element_type=jnp.float32).astype(
+            jnp.bfloat16
+        )
+
+    select_rows(0)
     barrier = pltpu.get_barrier_semaphore()
     for k in range(1, chips):
         pl.semaphore_signal(
@@ -112,12 +121,8 @@
         for s in range(streams)
     ]
     for s in range(streams):
-        state = state_ref[s].astype(jnp.float32)
-        scale = lax.rsqrt(jnp.mean(state * state, axis=-1, keepdims=True) + 1e-06)
-        normed = (state * scale * gain_ref[...]).astype(jnp.bfloat16)
-        xs[s] = jnp.dot(pick_ref[s], normed, preferred_element_type=jnp.float32).astype(
-            jnp.bfloat16
-        )
+        if s > 0:
+            select_rows(s)
         local_in[s].start()
         for k in range(1, chips):
             dispatch(s, k).start()

time: 188 us -> 188 us (level)
  no operation moved by 1% of the time
where the time goes in v11:
time: 188 us; the launch traced here: 187 us
  Pallas kernels  181 us (96%)
  local copies, waits for them, and re-layouts  4.07 us (2%)
    pallas_call x1, Pallas kernels, expert_pass(): pl.pallas_call(functools.partial(moe_kernel, chips), out_shape=jax.ShapeD...  181 us

profile of v11, /device:TPU:30, one launch (start us, length us, event | category | flops | bytes accessed | tf_op | source)
XLA Modules:
  0.0 186.6 jit_solution(1914462985393393446)
XLA Ops:
  0.0 0.8 copy.17
  0.8 0.1 eq.28
  0.9 0.2 convert_reduce_fusion
  1.1 0.1 reduce_sum.21
  1.3 0.1 copy.19
  1.4 0.1 fusion
  1.5 0.8 copy.20
  2.3 0.8 select_reduce_fusion
  3.1 0.7 subtract_convert_fusion
  3.8 180.7 %shard_map.73 = bf16[2,64,3584]{2,1,0:T(8,128)(2,1)} custom-call(bf16[3584,512]{1,0:T(8,128)(2,1)} %bitcast.12, bf16[3584,512]{1,0:T(8,128)(2,1)} %bitcast.13, bf16[512,3584]{1,0:T(8,128)(2,1)} %bitcast.14, bf16[2,64,3584]{2,1,0:T(8,128)(2,1)} %bitcast.15, f32[1,3584]{1,0:T(1,128)} %gain_ref.1, bf16[2,256,64]{2,1,0:T(8,128)(2,1)} %bitcast.16, ...), custom_call_target="tpu_custom_call" | custom-call | tf_op jit(solution)/shard_map/pallas_call | solution.py:191
  184.4 2.2 %copy.22 = bf16[1,2,64,3584]{3,2,1,0:T(8,128)(2,1)} copy(bf16[1,2,64,3584]{3,2,1,0:T(8,128)(2,1)} %bitcast.11) | data formatting | bytes 1835008
  (3 shorter events, 0.0 us)

commit v12 on v9

--- a/solution.py
+++ b/solution.py
@@ -103,6 +103,7 @@
             device_id=dev(q), device_id_type=MESH,
         )
 
+    farthest_first = sorted(range(1, chips), key=lambda k: -min(k, chips - k))
     local_in = [
         pltpu.make_async_copy(xs.at[s, blk(me)], recv.at[s, blk(me)], lsem.at[0, s])
         for s in range(streams)
@@ -119,7 +120,7 @@
             jnp.bfloat16
         )
         local_in[s].start()
-        for k in range(1, chips):
+        for k in farthest_first:
             dispatch(s, k).start()
     for c in to_sibling:
         c.start()
@@ -147,7 +148,7 @@
                 total = part if total is None else total + part
             res[s, pl.ds(b * tile, tile), :] = total.astype(jnp.bfloat16)
         local_out[s].start()
-        for k in range(1, chips):
+        for k in farthest_first:
             back(s, k).start()
 
     for s in range(streams):

time: 188 us -> 189 us (level)
  Pallas kernels: 181 us -> 183 us
    pallas_call x1, Pallas kernels: 181 us -> 183 us  [expert_pass(): pl.pallas_call(functools.partial(moe_kernel, chips), out_shape=jax.ShapeD...]
where the time goes in v12:
time: 189 us
  Pallas kernels  183 us (97%)
  local copies, waits for them, and re-layouts  4.07 us (2%)
    pallas_call x1, Pallas kernels, expert_pass(): pl.pallas_call(functools.partial(moe_kernel, chips), out_shape=jax.ShapeD...  183 us

profile of v12, /device:TPU:30, one launch (start us, length us, event | category | flops | bytes accessed | tf_op | source)
XLA Modules:
  0.0 189.0 jit_solution(11601192370301253299)
XLA Ops:
  0.0 0.8 copy.17
  0.8 0.1 eq.28
  0.9 0.2 convert_reduce_fusion
  1.1 0.1 reduce_sum.21
  1.3 0.1 copy.19
  1.4 0.1 fusion
  1.5 0.8 copy.20
  2.3 0.8 select_reduce_fusion
  3.1 0.7 subtract_convert_fusion
  3.8 183.1 %shard_map.73 = bf16[2,64,3584]{2,1,0:T(8,128)(2,1)} custom-call(bf16[3584,512]{1,0:T(8,128)(2,1)} %bitcast.12, bf16[3584,512]{1,0:T(8,128)(2,1)} %bitcast.13, bf16[512,3584]{1,0:T(8,128)(2,1)} %bitcast.14, bf16[2,64,3584]{2,1,0:T(8,128)(2,1)} %bitcast.15, f32[1,3584]{1,0:T(1,128)} %gain_ref.1, bf16[2,256,64]{2,1,0:T(8,128)(2,1)} %bitcast.16, ...), custom_call_target="tpu_custom_call" | custom-call | tf_op jit(solution)/shard_map/pallas_call | solution.py:187
  186.9 2.2 %copy.22 = bf16[1,2,64,3584]{3,2,1,0:T(8,128)(2,1)} copy(bf16[1,2,64,3584]{3,2,1,0:T(8,128)(2,1)} %bitcast.11) | data formatting | bytes 1835008
  (3 shorter events, 0.0 us)

commit v13 on v9

--- a/solution.py
+++ b/solution.py
@@ -130,7 +130,7 @@
     for c in to_sibling:
         c.wait_send()
 
-    tile = 128
+    tile = rows
     for s in range(streams):
         local_in[s].wait()
         for k in range(1, chips):

time: 188 us -> 188 us (level)
  no operation moved by 1% of the time
where the time goes in v13:
time: 188 us; the launch traced here: 187 us
  Pallas kernels  181 us (96%)
  local copies, waits for them, and re-layouts  4.07 us (2%)
    pallas_call x1, Pallas kernels, expert_pass(): pl.pallas_call(functools.partial(moe_kernel, chips), out_shape=jax.ShapeD...  181 us

profile of v13, /device:TPU:30, one launch (start us, length us, event | category | flops | bytes accessed | tf_op | source)
XLA Modules:
  0.0 186.7 jit_solution(3771873145170266657)
XLA Ops:
  0.0 0.8 copy.17
  0.8 0.1 eq.28
  0.9 0.2 convert_reduce_fusion
  1.1 0.1 reduce_sum.21
  1.3 0.1 copy.19
  1.4 0.1 fusion
  1.5 0.8 copy.20
  2.3 0.8 select_reduce_fusion
  3.1 0.7 subtract_convert_fusion
  3.8 180.7 %shard_map.73 = bf16[2,64,3584]{2,1,0:T(8,128)(2,1)} custom-call(bf16[3584,512]{1,0:T(8,128)(2,1)} %bitcast.12, bf16[3584,512]{1,0:T(8,128)(2,1)} %bitcast.13, bf16[512,3584]{1,0:T(8,128)(2,1)} %bitcast.14, bf16[2,64,3584]{2,1,0:T(8,128)(2,1)} %bitcast.15, f32[1,3584]{1,0:T(1,128)} %gain_ref.1, bf16[2,256,64]{2,1,0:T(8,128)(2,1)} %bitcast.16, ...), custom_call_target="tpu_custom_call" | custom-call | tf_op jit(solution)/shard_map/pallas_call | solution.py:186
  184.5 2.2 %copy.22 = bf16[1,2,64,3584]{3,2,1,0:T(8,128)(2,1)} copy(bf16[1,2,64,3584]{3,2,1,0:T(8,128)(2,1)} %bitcast.11) | data formatting | bytes 1835008
  (3 shorter events, 0.0 us)
